TPU v7x, 32 devices: a whole 2x2x4 slice. The times are simulated.
32 devices in a mesh: seq: 8 (over z, x), tp: 4 (over y, core).
Axes of the slice: x: 2, y: 2, z: 4, core: 2. Of those that a mesh axis runs over, the one named last changes fastest.
Arguments:
- tokens: bfloat16 [4096, 4096], P(('seq', 'tp')), may hold values from -64 to 64, as said below
- joined_projection_weight: bfloat16 [4096, 6144], P(None, 'tp'), may hold values from -0.09375 to 0.09375
- adapter_down_weight: bfloat16 [4096, 64], replicated, may hold values from -0.09375 to 0.09375
- adapter_up_weight: bfloat16 [64, 6144], P(None, 'tp'), may hold values from -0.75 to 0.75
- document_index: int32 [4096], replicated, may hold values from 0 to 3, as said below
- query_to_key_head: int32 [32], replicated, may hold values from 0 to 7, as said below
Outputs:
- context: bfloat16 [4096, 4096], P(('seq', 'tp'))
Inputs may be any that keep to these rules, and one draw needn't show every extreme that they name: `tokens`: rows of order one, except in the hidden draw where some rows have larger scales. `query_to_key_head`: each of 0 to 7 is named by exactly 4 query heads. `document_index`: never falling, starting at 0; each of the 4 documents covers 4096 / 16 or more positions.
All inputs are finite; a program needn't handle non-finite values.
Results may differ from a plain program's by a relative error of at most 0.012.
The roundings to bfloat16 on the way count: a program that leaves them out, or rounds other values in their place, can miss the bound.
Values may be sent and summed in bfloat16 or wider, within the bound.
A program may use at most 128 MiB of HBM per device.

v0:
```python
import jax
import jax.numpy as jnp
from jax import lax
from jax.sharding import PartitionSpec as P

H = 32
KV = 8
DH = 128


ADAPTER_SCALE = 0.5
THETA = 500000.0
NEG_BIG = -1e30


def rotate(values, places):
    half_dim = values.shape[-1] // 2
    frequency = THETA ** (-(jnp.arange(half_dim, dtype=jnp.float32) * 2.0) / values.shape[-1])
    angles = places[:, None] * frequency[None, :]
    cosine = jnp.cos(angles)[:, None, :]
    sine_part = jnp.sin(angles)[:, None, :]
    front_half = values[..., :half_dim]
    back_half = values[..., half_dim:]
    return jnp.concatenate(
        [front_half * cosine - back_half * sine_part, back_half * cosine + front_half * sine_part],
        axis=-1,
    )


def expand_heads(grouped, query_to_key_head):
    groups = grouped.shape[1]
    select = (query_to_key_head[None, :] == jnp.arange(groups, dtype=jnp.int32)[:, None]).astype(
        jnp.bfloat16
    )
    return jnp.einsum("tgd,gh->thd", grouped, select, preferred_element_type=jnp.float32).astype(
        jnp.bfloat16
    )


def per_device(
    tokens,
    joined_projection_weight,
    adapter_down_weight,
    adapter_up_weight,
    document_index,
    query_to_key_head,
):
    tp_count = lax.axis_size("tp")
    seq_count = lax.axis_size("seq")
    tp_rank = lax.axis_index("tp")
    seq_rank = lax.axis_index("seq")
    own_rows = tokens.shape[0]
    head_dim = DH
    query_local = H // tp_count
    kv_local = KV // tp_count
    collected_rows = lax.all_gather(tokens, "tp", axis=0, tiled=True)
    reduced_token_rows = jnp.dot(
        collected_rows, adapter_down_weight, preferred_element_type=jnp.float32
    ).astype(jnp.bfloat16)
    joined_output = jnp.dot(
        collected_rows, joined_projection_weight, preferred_element_type=jnp.float32
    )
    joined_output = joined_output + ADAPTER_SCALE * jnp.dot(
        reduced_token_rows, adapter_up_weight, preferred_element_type=jnp.float32
    )
    block_rows = collected_rows.shape[0]
    places = (seq_rank * block_rows + jnp.arange(block_rows, dtype=jnp.int32)).astype(jnp.float32)
    key_start_col = query_local * head_dim
    value_start_col = (query_local + kv_local) * head_dim
    queries = rotate(
        joined_output[:, :key_start_col].reshape(block_rows, query_local, head_dim), places
    ).astype(jnp.bfloat16)
    keys = rotate(
        joined_output[:, key_start_col:value_start_col].reshape(block_rows, kv_local, head_dim),
        places,
    ).astype(jnp.bfloat16)
    values_local = (
        joined_output[:, value_start_col:]
        .reshape(block_rows, kv_local, head_dim)
        .astype(jnp.bfloat16)
    )
    query_heads, key_group, value_group = (
        lax.all_to_all(queries, "tp", split_axis=0, concat_axis=1, tiled=True),
        lax.all_to_all(keys, "tp", split_axis=0, concat_axis=1, tiled=True),
        lax.all_to_all(values_local, "tp", split_axis=0, concat_axis=1, tiled=True),
    )
    key_heads = expand_heads(key_group, query_to_key_head)
    value_heads = expand_heads(value_group, query_to_key_head)
    query_shard, key_part, value_part = (
        lax.all_to_all(query_heads, "seq", split_axis=1, concat_axis=0, tiled=True),
        lax.all_to_all(key_heads, "seq", split_axis=1, concat_axis=0, tiled=True),
        lax.all_to_all(value_heads, "seq", split_axis=1, concat_axis=0, tiled=True),
    )
    heads_part = key_part.shape[1]
    key_blocks = key_part.reshape(seq_count, 1, own_rows, heads_part, head_dim)
    value_blocks = value_part.reshape(seq_count, 1, own_rows, heads_part, head_dim)
    key_whole, value_whole = (
        lax.all_gather(key_blocks, "tp", axis=1, tiled=True),
        lax.all_gather(value_blocks, "tp", axis=1, tiled=True),
    )
    key_shard = key_whole.reshape(-1, heads_part, head_dim)
    value_shard = value_whole.reshape(-1, heads_part, head_dim)
    query_count = query_shard.shape[0]
    heads_here = query_shard.shape[1]
    query_block = min(1024, query_count)
    key_block = 2 * query_block
    per_block = query_block * tp_count // key_block
    local_index = jnp.arange(query_count, dtype=jnp.int32)
    query_places = (
        local_index // own_rows * block_rows + tp_rank * own_rows + local_index % own_rows
    )
    query_segments = jnp.take(document_index, query_places)
    scale = head_dim ** (-0.5)

    def attend_block(block_index):
        start = block_index * query_block
        query_tile = lax.dynamic_slice_in_dim(query_shard, start, query_block, 0)
        tile_places = lax.dynamic_slice_in_dim(query_places, start, query_block, 0)
        tile_segments = lax.dynamic_slice_in_dim(query_segments, start, query_block, 0)

        def key_step(key_index, carry):
            running_max, running_sum, accumulated = carry
            key_start = key_index * key_block
            key_tile = lax.dynamic_slice_in_dim(key_shard, key_start, key_block, 0)
            value_tile = lax.dynamic_slice_in_dim(value_shard, key_start, key_block, 0)
            key_places = key_start + jnp.arange(key_block, dtype=jnp.int32)
            key_segments = lax.dynamic_slice_in_dim(document_index, key_start, key_block, 0)
            scores = (
                jnp.einsum("qhd,khd->qhk", query_tile, key_tile, preferred_element_type=jnp.float32)
                * scale
            )
            allowed = (key_places[None, :] <= tile_places[:, None]) & (
                key_segments[None, :] == tile_segments[:, None]
            )
            scores = jnp.where(allowed[:, None, :], scores, -jnp.inf)
            new_max = jnp.maximum(running_max, jnp.max(scores, axis=-1))
            factor = jnp.exp(running_max - new_max)
            powers = jnp.exp(scores - new_max[..., None])
            running_sum = running_sum * factor + jnp.sum(powers, axis=-1)
            update = jnp.einsum(
                "qhk,khd->qhd",
                powers.astype(jnp.bfloat16),
                value_tile,
                preferred_element_type=jnp.float32,
            )
            accumulated = accumulated * factor[..., None] + update
            return (new_max, running_sum, accumulated)

        initial = (
            jnp.full((query_block, heads_here), NEG_BIG, jnp.float32),
            jnp.zeros((query_block, heads_here), jnp.float32),
            jnp.zeros((query_block, heads_here, head_dim), jnp.float32),
        )
        final_max, final_sum, accumulated = lax.fori_loop(
            0, (block_index + 1) * per_block, key_step, initial
        )
        return (accumulated / final_sum[..., None]).astype(jnp.bfloat16)

    tiles = lax.map(attend_block, jnp.arange(query_count // query_block, dtype=jnp.int32))
    context_heads = tiles.reshape(query_count, heads_here, head_dim)
    context_rows = lax.all_to_all(context_heads, "seq", split_axis=0, concat_axis=1, tiled=True)
    return context_rows.reshape(own_rows, -1)


def solution(mesh):
    return jax.shard_map(
        per_device,
        mesh=mesh,
        in_specs=(P(("seq", "tp"), None), P(None, "tp"), P(), P(None, "tp"), P(), P()),
        out_specs=P(("seq", "tp"), None),
        check_vma=False,
    )
```

profile of v0, /device:TPU:10, one launch (start us, length us, event | category | flops | bytes accessed | tf_op | source)
XLA Modules:
  0.0 364.1 jit_solution(15220378711317120716)
XLA Ops:
  6.5 0.7 all-gather.6.cloned.1.call-update
  7.3 1.0 multiply_cosine_fusion
  8.3 36.2 %all-gather.6.cloned.1.call-done = bf16[512,4096]{1,0:T(8,128)(2,1)} async-done(((bf16[128,4096]{1,0:T(8,128)(2,1)}), bf16[512,4096]{1,0:T(8,128)(2,1)}) %all-gather.6.cloned.1.call-update) | async-done | bytes 4194320 | tf_op jit(solution)/shard_map/all_gather | solution.py:56
  44.5 12.2 %fusion.51 = f32[512,1536]{1,0:T(8,128)} fusion(bf16[512,4096]{1,0:T(8,128)(2,1)} %all-gather.6.cloned.1.call-done, bf16[4096,1536]{1,0:T(8,128)(2,1)} %param.9), kind=kOutput, calls=%fused_computation.91 | convolution fusion | flops 6442450944 | bytes 19922944 | tf_op jit(solution)/shard_map/dot_general | solution.py:60
  56.7 6.9 %fusion.30 = f32[512,1536]{1,0:T(8,128)} fusion(f32[512,1536]{1,0:T(8,128)} %fusion.51, bf16[64,1536]{1,0:T(8,128)(2,1)S(1)} %copy-done.3, bf16[512,4096]{1,0:T(8,128)(2,1)} %all-gather.6.cloned.1.call-done, bf16[4096,64]{0,1:T(8,128)(2,1)S(1)} %copy-done), kind=kOutput, calls=%fused_computation.39 | convolution fusion | flops 370704384 | bytes 11206656 | tf_op jit(solution)/shard_map/dot_general | solution.py:63
  63.6 1.1 slice.31
  64.7 0.3 reshape.214
  64.9 0.8 subtract_convert_fusion.1
  65.7 0.7 pad_maximum_fusion.1
  66.4 8.4 %all_to_all.117 = bf16[512,2,128]{2,1,0:T(2,128)(2,1)S(1)} all-to-all(bf16[512,2,128]{2,1,0:T(2,128)(2,1)S(1)} %pad_maximum_fusion.1), channel_id=1, replica_groups=mesh['seq'=8,'tp'=4] {'tp'}, dimensions={0} | all-to-all | bytes 524288 | tf_op jit(solution)/shard_map/all_to_all | solution.py:84
  74.8 0.2 copy.43
  75.0 0.5 fusion.31
  75.5 0.4 copy.44
  75.9 29.1 %all_to_all.118 = bf16[128,32,128]{2,0,1:T(8,128)(2,1)S(1)} all-to-all(bf16[128,32,128]{2,0,1:T(8,128)(2,1)S(1)} %copy.44), channel_id=1, replica_groups=mesh['seq'=8,'tp'=4] {'seq'}, dimensions={1} | all-to-all | bytes 2097152 | tf_op jit(solution)/shard_map/all_to_all | solution.py:91
  105.0 1.6 copy.66
  106.7 1.1 slice.48
  107.9 8.4 %all_to_all.119 = bf16[512,2,128]{2,1,0:T(2,128)(2,1)S(1)} all-to-all(bf16[512,2,128]{2,1,0:T(2,128)(2,1)S(1)} %convert_element_type.42), channel_id=1, replica_groups=mesh['seq'=8,'tp'=4] {'tp'}, dimensions={0} | all-to-all | bytes 524288 | tf_op jit(solution)/shard_map/all_to_all | solution.py:85
  116.4 0.5 fusion.32
  116.9 0.4 copy.51
  117.3 29.1 %all_to_all.120 = bf16[128,32,128]{2,0,1:T(8,128)(2,1)S(1)} all-to-all(bf16[128,32,128]{2,0,1:T(8,128)(2,1)S(1)} %copy.51), channel_id=1, replica_groups=mesh['seq'=8,'tp'=4] {'seq'}, dimensions={1} | all-to-all | bytes 2097152 | tf_op jit(solution)/shard_map/all_to_all | solution.py:92
  146.4 1.7 copy.64
  148.1 1.7 slice_bitcast_fusion
  149.8 0.5 copy.60
  150.3 0.9 subtract_convert_fusion
  151.2 0.6 pad_maximum_fusion
  151.8 27.6 %all_to_all.121 = bf16[512,8,128]{2,1,0:T(8,128)(2,1)S(1)} all-to-all(bf16[512,8,128]{2,1,0:T(8,128)(2,1)S(1)} %pad_maximum_fusion), channel_id=1, replica_groups=mesh['seq'=8,'tp'=4] {'tp'}, dimensions={0} | all-to-all | bytes 2097152 | tf_op jit(solution)/shard_map/all_to_all | solution.py:83
  179.6 1.4 copy.48
  180.9 6.4 %all-to-all-start.3 = ((bf16[128,32,128]{2,0,1:T(8,128)(2,1)}), bf16[128,32,128]{2,0,1:T(8,128)(2,1)S(1)}, u32[]{:S(2)}, u32[]{:S(2)}) async-start(bf16[128,32,128]{2,0,1:T(8,128)(2,1)} %copy.48), calls=%async_computation.3 | async-start | bytes 2097152 | tf_op jit(solution)/shard_map/all_to_all | solution.py:90
  187.4 6.2 %gather_fusion = s32[1024]{0:T(1024)S(1)} fusion(s32[4096]{0:T(1024)S(1)} %copy-done.2, s32[1024]{0:T(1024)S(1)} %broadcast_clamp_fusion), kind=kCustom, calls=%fused_computation | custom fusion | bytes 12288 | tf_op jit(solution)/shard_map/jit(_take)/gather | solution.py:112
  193.5 16.2 %all-to-all-done.3 = bf16[128,32,128]{2,0,1:T(8,128)(2,1)S(1)} async-done(((bf16[128,32,128]{2,0,1:T(8,128)(2,1)}), bf16[128,32,128]{2,0,1:T(8,128)(2,1)S(1)}, u32[]{:S(2)}, u32[]{:S(2)}) %all-to-all-start.3) | async-done | bytes 1048608 | tf_op jit(solution)/shard_map/all_to_all | solution.py:90
  209.7 1.0 copy.49
  210.8 5.9 %copy.46 = bf16[8,512,4,128]{3,1,0,2:T(8,128)(2,1)} copy(bf16[8,512,4,128]{3,0,2,1:T(8,128)(2,1)} %all-gather.8.cloned.1.call-done) | data formatting | bytes 8388608 | tf_op jit(solution)/shard_map/all_gather | solution.py:98
  216.6 5.8 %copy.53 = bf16[8,512,4,128]{3,1,0,2:T(8,128)(2,1)} copy(bf16[8,512,4,128]{3,0,2,1:T(8,128)(2,1)} %all-gather.10.cloned.1.call-done) | data formatting | bytes 8388608 | tf_op jit(solution)/shard_map/all_gather | solution.py:99
  222.4 98.0 %while.24 = (s32[]{:T(128)}, f32[1024,4]{0,1:T(4,128)S(1)}, f32[1024,4]{0,1:T(4,128)S(1)}, f32[1024,4,128]{0,2,1:T(8,128)}, s32[4096]{0:T(1024)S(1)}, /*index=5*...) while((s32[]{:T(128)}, f32[1024,4]{0,1:T(4,128)S(1)}, ...), condition=%wide.region_3.4_spmd.clone, body=%wide.region_0.3_spmd.clone.sunk | while | flops 4395144192 | bytes 118804696 | solution.py:154
  222.4 2.3 compare_and_fusion.2
  224.8 15.1 %fusion.71 = (f32[1024,4]{0,1:T(4,128)S(1)}, f32[4,2048,1024]{2,1,0:T(8,128)}) fusion(pred[1024,2048]{0,1:T(8,128)(4,1)S(1)} %compare_and_fusion.2, bf16[1024,4,128]{2,0,1:T(8,128)(2,1)} %get-tuple-element.290, bf16[4096,4,128]{2,0,1:T(8,128)(2,1)} %get-tuple-element.289, s32[]{:T(128)S(6)} %select_n.149), kind=kOutput, calls=%fused_computation.6.clone.1 | convolution fusion | flops 2172645376 | bytes 38813700 | tf_op jit(solution)/shard_map/while/body/eval_jaxpr/while/body/qhd,khd->qhk/dot_general | solution.py:129
  239.9 14.3 %fusion.72 = f32[1024,4]{0,1:T(4,128)S(1)} fusion(f32[4,2048,1024]{2,1,0:T(8,128)} %get-tuple-element.252, f32[1024,4]{0,1:T(4,128)S(1)} %select_maximum_fusion.2, pred[1024,2048]{0,1:T(8,128)(4,1)S(1)} %compare_and_fusion.2), kind=kLoop, calls=%fused_computation.5.clone.1 | loop fusion | flops 33550336 | bytes 35684352 | tf_op jit(solution)/shard_map/while/body/eval_jaxpr/while/body/reduce_sum | solution.py:139
  254.3 16.9 %bitcast_add_fusion.2 = f32[1024,4,128]{0,2,1:T(8,128)} fusion(f32[1024,4,128]{0,2,1:T(8,128)} %get-tuple-element.272, f32[4,2048,1024]{2,1,0:T(8,128)} %get-tuple-element.252, f32[1024,4]{0,1:T(4,128)S(1)} %select_maximum_fusion.2, pred[1024,2048]{0,1:T(8,128)(4,1)S(1)} %compare_and_fusion.2, bf16[4096,4,128]{2,0,1:T(8,128)(2,1)} %get-tuple-element.291, ...), kind=kOutput, calls=%fused_computation.10.clone.1 | convolution fusion | flops 2182610944 | bytes 41975812 | tf_op jit(solution)/shard_map/while/body/eval_jaxpr/while/body/qhk,khd->qhd/dot_general | solution.py:140
  271.2 2.3 compare_and_fusion.2
  273.6 15.1 %fusion.71 = (f32[1024,4]{0,1:T(4,128)S(1)}, f32[4,2048,1024]{2,1,0:T(8,128)}) fusion(pred[1024,2048]{0,1:T(8,128)(4,1)S(1)} %compare_and_fusion.2, bf16[1024,4,128]{2,0,1:T(8,128)(2,1)} %get-tuple-element.290, bf16[4096,4,128]{2,0,1:T(8,128)(2,1)} %get-tuple-element.289, s32[]{:T(128)S(6)} %select_n.149), kind=kOutput, calls=%fused_computation.6.clone.1 | convolution fusion | flops 2172645376 | bytes 38813700 | tf_op jit(solution)/shard_map/while/body/eval_jaxpr/while/body/qhd,khd->qhk/dot_general | solution.py:129
  288.7 14.3 %fusion.72 = f32[1024,4]{0,1:T(4,128)S(1)} fusion(f32[4,2048,1024]{2,1,0:T(8,128)} %get-tuple-element.252, f32[1024,4]{0,1:T(4,128)S(1)} %select_maximum_fusion.2, pred[1024,2048]{0,1:T(8,128)(4,1)S(1)} %compare_and_fusion.2), kind=kLoop, calls=%fused_computation.5.clone.1 | loop fusion | flops 33550336 | bytes 35684352 | tf_op jit(solution)/shard_map/while/body/eval_jaxpr/while/body/reduce_sum | solution.py:139
  303.1 17.4 %bitcast_add_fusion.2 = f32[1024,4,128]{0,2,1:T(8,128)} fusion(f32[1024,4,128]{0,2,1:T(8,128)} %get-tuple-element.272, f32[4,2048,1024]{2,1,0:T(8,128)} %get-tuple-element.252, f32[1024,4]{0,1:T(4,128)S(1)} %select_maximum_fusion.2, pred[1024,2048]{0,1:T(8,128)(4,1)S(1)} %compare_and_fusion.2, bf16[4096,4,128]{2,0,1:T(8,128)(2,1)} %get-tuple-element.291, ...), kind=kOutput, calls=%fused_computation.10.clone.1 | convolution fusion | flops 2182610944 | bytes 41975812 | tf_op jit(solution)/shard_map/while/body/eval_jaxpr/while/body/qhk,khd->qhd/dot_general | solution.py:140
  320.5 0.2 copy.55
  320.7 2.0 copy.56
  322.7 2.5 divide_convert_fusion
  325.2 30.4 %all_to_all.122 = bf16[1024,4,128]{2,1,0:T(4,128)(2,1)S(1)} all-to-all(bf16[1024,4,128]{2,1,0:T(4,128)(2,1)S(1)} %divide_convert_fusion), channel_id=1, replica_groups=mesh['seq'=8,'tp'=4] {'seq'}, dimensions={0} | all-to-all | bytes 2097152 | tf_op jit(solution)/shard_map/all_to_all | solution.py:161
  355.6 0.4 copy.57
  356.0 1.6 reshape.220
  (40 shorter events, 0.7 us)
Async XLA Ops:
  6.5 50.1 %copy-start = (bf16[4096,64]{0,1:T(8,128)(2,1)S(1)}, bf16[4096,64]{0,1:T(8,128)(2,1)}, u32[]{:S(2)}) copy-start(bf16[4096,64]{0,1:T(8,128)(2,1)} %param.10) | copy-start | bytes 1572868
  6.5 38.0 %all-gather.6.cloned.1.call-start = ((), (), s32[]{:S(2)}) async-start(), calls=%async_computation.7 | async-start | bytes 5242880 | tf_op jit(solution)/shard_map/all_gather | solution.py:56
  7.3 203.5 %all-gather.8.cloned.1.call-start = ((), (), s32[]{:S(2)}) async-start(), calls=%async_computation.8 | async-start | bytes 5242880 | tf_op jit(solution)/shard_map/all_gather | solution.py:98
  8.3 48.4 %copy-start.3 = (bf16[64,1536]{1,0:T(8,128)(2,1)S(1)}, bf16[64,1536]{1,0:T(8,128)(2,1)}, u32[]{:S(2)}) copy-start(bf16[64,1536]{1,0:T(8,128)(2,1)} %param.11) | copy-start | bytes 589828
  63.6 11.5 %copy-start.4 = (s32[32]{0:T(128)S(1)}, s32[32]{0:T(128)}, u32[]{:S(2)}) copy-start(s32[32]{0:T(128)} %param.13) | copy-start | bytes 388
  106.7 110.0 %all-gather.10.cloned.1.call-start = ((), (), s32[]{:S(2)}) async-start(), calls=%async_computation.9 | async-start | bytes 5242880 | tf_op jit(solution)/shard_map/all_gather | solution.py:99
  179.4 8.0 %copy-start.2 = (s32[4096]{0:T(1024)S(1)}, s32[4096]{0:T(1024)}, u32[]{:S(2)}) copy-start(s32[4096]{0:T(1024)} %param.12) | copy-start | bytes 49156
  180.9 28.8 %all-to-all-start.3 = ((bf16[128,32,128]{2,0,1:T(8,128)(2,1)}), bf16[128,32,128]{2,0,1:T(8,128)(2,1)S(1)}, u32[]{:S(2)}, u32[]{:S(2)}) async-start(bf16[128,32,128]{2,0,1:T(8,128)(2,1)} %copy.48), calls=%async_computation.3 | async-start | bytes 2097152 | tf_op jit(solution)/shard_map/all_to_all | solution.py:90
  322.7 34.9 %copy-start.1 = (bf16[4096,64]{0,1:T(8,128)(2,1)S(1)}, bf16[4096,64]{0,1:T(8,128)(2,1)}, u32[]{:S(2)}) copy-start(bf16[4096,64]{0,1:T(8,128)(2,1)} %param.10) | copy-start | bytes 1572868
Sparse Core Ops, SparseCore 0:
  8.9 35.5 all-gather.5
  106.8 34.4 all-gather.7
  148.2 44.4 all-gather.9
where the time goes:
time: 368 us; the launch traced here: 364 us
  blocking collectives  133 us (36%)
  matrix products  84.5 us (23%)
  waiting for transfers between devices  53.1 us (14%)
  other arithmetic  39.9 us (11%)
  local copies, waits for them, and re-layouts  33.8 us (9%)
  between operations  13.3 us (4%)
  starting transfers between devices  6.46 us (2%)
    all_gather x1, waiting for transfers between devices, per_device(): collected_rows = lax.all_gather(tokens, 'tp', axis=0, tiled=True)  36.2 us
    dot_general x2, matrix products, key_step(): jnp.einsum('qhk,khd->qhd', powers.astype(jnp.bfloat16), value_tile, prefe...  34.2 us
    all_to_all x1, blocking collectives, per_device(): lax.all_to_all(context_heads, 'seq', split_axis=0, concat_axis=1, tiled=T...  30.4 us
    dot_general x2, matrix products, key_step(): jnp.einsum('qhd,khd->qhk', query_tile, key_tile, preferred_element_type=j...  30.3 us
    all_to_all x1, blocking collectives, per_device(): lax.all_to_all(value_heads, 'seq', split_axis=1, concat_axis=0, tiled=True)  29.1 us
    all_to_all x1, blocking collectives, per_device(): lax.all_to_all(key_heads, 'seq', split_axis=1, concat_axis=0, tiled=True)  29.1 us
    reduce_sum x2, other arithmetic, key_step(): running_sum = running_sum * factor + jnp.sum(powers, axis=-1)  28.7 us
    all_to_all x1, blocking collectives, per_device(): lax.all_to_all(queries, 'tp', split_axis=0, concat_axis=1, tiled=True)  27.6 us
  transfers between devices with their start and end apart: 4, of which 2 were waited for; matrix products, arithmetic and copies ran while one was open for 6% of the time, Pallas kernels for 0%

commit v1 on v0

v1 whole, which is shorter than its diff:
```python
import functools

import jax
import jax.numpy as jnp
from jax import lax
from jax.experimental import pallas as pl
from jax.experimental.pallas import tpu as pltpu
from jax.sharding import PartitionSpec as P

H = 32
KV = 8
DH = 128
GROUP = H // KV

ADAPTER_SCALE = 0.5
THETA = 500000.0
NEG_BIG = -1e30
LOG2_E = 1.4426950408889634


def rope_tables(places):
    half = DH // 2
    frequency = THETA ** (-(jnp.arange(half, dtype=jnp.float32) * 2.0) / DH)
    angles = places[:, None] * frequency[None, :]
    cosine, sine = jnp.cos(angles), jnp.sin(angles)
    return jnp.concatenate([cosine, cosine], 1), jnp.concatenate([-sine, sine], 1)


def project_kernel(rotated_pairs, x_ref, w_ref, down_ref, up_ref, cos_ref, sin_ref, out_ref, mid_ref):
    step = pl.program_id(0)
    chunks, pair, rows, _ = out_ref.shape

    @pl.when(step == 0)
    def _():
        mid_ref[...] = jnp.dot(
            x_ref[...], down_ref[...], preferred_element_type=jnp.float32
        ).astype(jnp.bfloat16)

    joined = jnp.dot(x_ref[...], w_ref[...], preferred_element_type=jnp.float32)
    joined = joined + ADAPTER_SCALE * jnp.dot(
        mid_ref[...], up_ref[...], preferred_element_type=jnp.float32
    )

    def store(head, value):
        value = value.astype(jnp.bfloat16)
        for chunk in range(chunks):
            out_ref[chunk, head] = value[chunk * rows : (chunk + 1) * rows]

    @pl.when(step < rotated_pairs)
    def _():
        for head in range(pair):
            part = joined[:, head * DH : (head + 1) * DH]
            store(head, part * cos_ref[...] + pltpu.roll(part, DH // 2, 1) * sin_ref[...])

    @pl.when(step >= rotated_pairs)
    def _():
        for head in range(pair):
            store(head, joined[:, head * DH : (head + 1) * DH])


def project(x, w, down, up, cosine, sine, tp_count, rotated_heads):
    rows, width = x.shape
    heads = w.shape[1] // DH
    pair = 2
    own = rows // tp_count
    return pl.pallas_call(
        functools.partial(project_kernel, rotated_heads // pair),
        grid=(heads // pair,),
        in_specs=[
            pl.BlockSpec((rows, width), lambda i: (0, 0)),
            pl.BlockSpec((width, pair * DH), lambda i: (0, i)),
            pl.BlockSpec(down.shape, lambda i: (0, 0)),
            pl.BlockSpec((up.shape[0], pair * DH), lambda i: (0, i)),
            pl.BlockSpec((rows, DH), lambda i: (0, 0)),
            pl.BlockSpec((rows, DH), lambda i: (0, 0)),
        ],
        out_specs=pl.BlockSpec((tp_count, pair, own, DH), lambda i: (0, i, 0, 0)),
        out_shape=jax.ShapeDtypeStruct((tp_count, heads, own, DH), jnp.bfloat16),
        scratch_shapes=[pltpu.VMEM((rows, down.shape[1]), jnp.bfloat16)],
        name="project",
    )(x, w, down, up, cosine, sine)


def select_kernel(index_ref, in_ref, out_ref):
    @pl.loop(0, out_ref.shape[0])
    def _(slot):
        out_ref[slot] = in_ref[index_ref[slot]]


def select(index, slabs):
    return pl.pallas_call(
        select_kernel,
        in_specs=[pl.BlockSpec(memory_space=pltpu.SMEM), pl.BlockSpec(memory_space=pltpu.VMEM)],
        out_specs=pl.BlockSpec(memory_space=pltpu.VMEM),
        out_shape=jax.ShapeDtypeStruct((index.shape[0],) + slabs.shape[1:], slabs.dtype),
        name="select_heads",
    )(index, slabs)


def merge_kernel(index_ref, in_ref, out_ref):
    for head in range(in_ref.shape[0]):
        out_ref[:, head * DH : (head + 1) * DH] = in_ref[index_ref[head]]


def merge(index, slabs):
    heads, rows, _ = slabs.shape
    return pl.pallas_call(
        merge_kernel,
        in_specs=[pl.BlockSpec(memory_space=pltpu.SMEM), pl.BlockSpec(memory_space=pltpu.VMEM)],
        out_specs=pl.BlockSpec(memory_space=pltpu.VMEM),
        out_shape=jax.ShapeDtypeStruct((rows, heads * DH), slabs.dtype),
        name="merge_heads",
    )(index, slabs)


def attend_kernel(heads, first_ref, place_ref, q_ref, kv_ref, begin_ref, out_ref):
    step = pl.program_id(0)
    chunks, _, _, own, _ = kv_ref.shape
    block = chunks * own
    rows = heads * own
    q = q_ref[0, :heads].reshape(rows, DH)
    place = place_ref[step]
    begins = jnp.concatenate([begin_ref[...]] * heads, 0)
    places = place + lax.broadcasted_iota(jnp.int32, (own, 1), 0)
    places = jnp.concatenate([places] * heads, 0)
    factor = (DH**-0.5) * LOG2_E

    def body(index, carry):
        top, total, acc = carry
        keys = kv_ref[:, index, 0].reshape(block, DH)
        values = kv_ref[:, index, 1].reshape(block, DH)
        scores = lax.dot_general(
            q, keys, (((1,), (1,)), ((), ())), preferred_element_type=jnp.float32
        )
        at = index * block + lax.broadcasted_iota(jnp.int32, (1, block), 1)
        scores = jnp.where((at <= places) & (at >= begins), scores, NEG_BIG)
        new_top = jnp.maximum(top, jnp.max(scores, 1, keepdims=True))
        shrink = jnp.exp2((top - new_top) * factor)
        powers = jnp.exp2((scores - new_top) * factor)
        total = total * shrink + jnp.sum(powers, 1, keepdims=True)
        acc = acc * shrink + jnp.dot(
            powers.astype(jnp.bfloat16), values, preferred_element_type=jnp.float32
        )
        return new_top, total, acc

    last = place // block
    start = (
        jnp.full((rows, 1), NEG_BIG, jnp.float32),
        jnp.zeros((rows, 1), jnp.float32),
        jnp.zeros((rows, DH), jnp.float32),
    )
    carry = body(last, start)
    top, total, acc = lax.fori_loop(first_ref[step] // block, last, body, carry)
    out_ref[0] = (acc / total).astype(jnp.bfloat16).reshape(heads, own, DH)


def attend(first, place, q, kv, begins, heads):
    steps, slabs, own, _ = q.shape
    return pl.pallas_call(
        functools.partial(attend_kernel, heads),
        grid_spec=pltpu.PrefetchScalarGridSpec(
            num_scalar_prefetch=2,
            grid=(steps,),
            in_specs=[
                pl.BlockSpec((1, slabs, own, DH), lambda i, *_: (i, 0, 0, 0)),
                pl.BlockSpec(kv.shape, lambda i, *_: (0,) * 5),
                pl.BlockSpec((own, 1), lambda i, *_: (i, 0)),
            ],
            out_specs=pl.BlockSpec((1, heads, own, DH), lambda i, *_: (i, 0, 0, 0)),
        ),
        out_shape=jax.ShapeDtypeStruct((steps, heads, own, DH), jnp.bfloat16),
        name="attend",
    )(first, place, q, kv, begins)


def head_tables(query_to_key_head, tp_count, seq_count):
    heads = jnp.arange(H, dtype=jnp.int32)
    same = query_to_key_head[:, None] == query_to_key_head[None, :]
    earlier = heads[None, :] < heads[:, None]
    slot = GROUP * query_to_key_head + jnp.sum((same & earlier).astype(jnp.int32), 1)
    order = jnp.sum(jnp.where(slot[None, :] == heads[:, None], heads[None, :], 0), 1)
    q_per, kv_per = H // tp_count, KV // tp_count
    local = q_per + 2 * kv_per
    here = H // seq_count
    q_index = (order // q_per * local + order % q_per).reshape(seq_count, here)
    kv_head = jnp.arange(seq_count, dtype=jnp.int32) * here // GROUP
    k_index = kv_head // kv_per * local + q_per + kv_head % kv_per
    index = jnp.concatenate([q_index, k_index[:, None], k_index[:, None] + kv_per], 1)
    return index.reshape(-1).astype(jnp.int32), slot.astype(jnp.int32)


def per_device(
    tokens,
    joined_projection_weight,
    adapter_down_weight,
    adapter_up_weight,
    document_index,
    query_to_key_head,
):
    tp_count = lax.axis_size("tp")
    seq_count = lax.axis_size("seq")
    tp_rank = lax.axis_index("tp")
    seq_rank = lax.axis_index("seq")
    own = tokens.shape[0]
    block = own * tp_count
    here = H // seq_count
    q_per, kv_per = H // tp_count, KV // tp_count

    index, slot = head_tables(query_to_key_head, tp_count, seq_count)
    places = (seq_rank * block + jnp.arange(block, dtype=jnp.int32)).astype(jnp.float32)
    cosine, sine = rope_tables(places)
    first_place = jnp.arange(seq_count, dtype=jnp.int32) * block + tp_rank * own
    all_places = jnp.arange(document_index.shape[0], dtype=jnp.int32)
    starts_here = jnp.concatenate(
        [jnp.ones((1,), jnp.bool_), document_index[1:] != document_index[:-1]]
    )
    begin = lax.cummax(jnp.where(starts_here, all_places, 0))
    begin = lax.dynamic_slice_in_dim(
        begin.reshape(seq_count, tp_count, own), tp_rank, 1, 1
    ).reshape(seq_count, own)

    rows = lax.all_gather(tokens, "tp", axis=0, tiled=True)
    heads = project(
        rows, joined_projection_weight, adapter_down_weight, adapter_up_weight,
        cosine, sine, tp_count, q_per + kv_per,
    )
    heads = lax.all_to_all(heads, "tp", split_axis=0, concat_axis=0, tiled=True)
    sent = select(index, heads.reshape(-1, own, DH)).reshape(seq_count, here + 2, own, DH)
    held = lax.all_to_all(sent, "seq", split_axis=0, concat_axis=0, tiled=True)
    kv = lax.all_gather(held[:, here:], "tp", axis=0)
    context = attend(
        begin[:, 0], first_place, held, kv, begin.reshape(seq_count * own, 1), here
    )
    context = lax.all_to_all(context, "seq", split_axis=0, concat_axis=0, tiled=True)
    return merge(slot, context.reshape(H, own, DH))


def solution(mesh):
    return jax.shard_map(
        per_device,
        mesh=mesh,
        in_specs=(P(("seq", "tp"), None), P(None, "tp"), P(), P(None, "tp"), P(), P()),
        out_specs=P(("seq", "tp"), None),
        check_vma=False,
    )
```

time: 368 us -> 214 us (0.58)
  matrix products: 84.5 us -> 0 us
  blocking collectives: 133 us -> 70.3 us
  Pallas kernels: 0 us -> 40.8 us
  other arithmetic: 39.9 us -> 3.63 us
  local copies, waits for them, and re-layouts: 33.8 us -> 7.14 us
  waiting for transfers between devices: 53.1 us -> 71.8 us
    dot_general x8 -> x0, matrix products: 84.5 us -> none  [the longest x2 34.2 us: key_step(): jnp.einsum('qhk,khd->qhd', powers.astype(jnp.bfloat16), value_tile, prefe...]
    all_to_all x6 -> x2, blocking collectives: 133 us -> 70.3 us  [the longest x1 40.6 us: per_device(): held = lax.all_to_all(sent, 'seq', split_axis=0, concat_axis=0, tiled=True)]
    pallas_call x0 -> x4, Pallas kernels: none -> 40.8 us  [the longest x1 20.9 us: attend(): pl.pallas_call(functools.partial(attend_kernel, heads), grid_spec=pltpu.P...]
    reduce_sum x2, other arithmetic: 28.7 us -> 0.29 us  [the longest x1 0.18 us: head_tables(): jnp.sum((same & earlier).astype(jnp.int32), 1)]
    all_gather x3 -> x2, waiting for transfers between devices: 36.2 us -> 52.3 us  [the longest x1 32.9 us: per_device(): rows = lax.all_gather(tokens, 'tp', axis=0, tiled=True)]
    all_gather x2 -> x0, local copies, waits for them, and re-layouts: 11.6 us -> none  [the longest x1 5.86 us: per_device(): lax.all_gather(key_blocks, 'tp', axis=1, tiled=True)]
    all_to_all x8 -> x0, local copies, waits for them, and re-layouts: 6.62 us -> none  [the longest x1 1.67 us: per_device(): lax.all_to_all(value_heads, 'seq', split_axis=1, concat_axis=0, tiled=True)]
    gather x1 -> x0, local copies, waits for them, and re-layouts: 6.15 us -> none  [per_device(): query_segments = jnp.take(document_index, query_places)]
  transfers between devices with their start and end apart: 4 -> 3, of which waited for: 2 -> 3; matrix products, arithmetic and copies ran while one was open for 6% -> 4% of each run, Pallas kernels for 0% -> 0%
where the time goes in v1:
time: 214 us; the launch traced here: 211 us
  waiting for transfers between devices  71.8 us (34%)
  blocking collectives  70.3 us (33%)
  Pallas kernels  40.8 us (19%)
  between operations  13.5 us (6%)
  local copies, waits for them, and re-layouts  7.14 us (3%)
  starting transfers between devices  3.74 us (2%)
  other arithmetic  3.63 us (2%)
    all_to_all x1, blocking collectives, per_device(): held = lax.all_to_all(sent, 'seq', split_axis=0, concat_axis=0, tiled=True)  40.6 us
    all_gather x1, waiting for transfers between devices, per_device(): rows = lax.all_gather(tokens, 'tp', axis=0, tiled=True)  32.9 us
    all_to_all x1, blocking collectives, per_device(): lax.all_to_all(context, 'seq', split_axis=0, concat_axis=0, tiled=True)  29.7 us
    pallas_call x1, Pallas kernels, attend(): pl.pallas_call(functools.partial(attend_kernel, heads), grid_spec=pltpu.P...  20.9 us
    all_gather x1, waiting for transfers between devices, per_device(): kv = lax.all_gather(held[:, here:], 'tp', axis=0)  19.4 us
    all_to_all x1, waiting for transfers between devices, per_device(): heads = lax.all_to_all(heads, 'tp', split_axis=0, concat_axis=0, tiled=True)  18.8 us
    pallas_call x1, Pallas kernels, project(): pl.pallas_call(functools.partial(project_kernel, rotated_heads // pair),...  14.5 us
  transfers between devices with their start and end apart: 3, of which 3 were waited for; matrix products, arithmetic and copies ran while one was open for 4% of the time, Pallas kernels for 0%

profile of v1, /device:TPU:10, one launch (start us, length us, event | category | flops | bytes accessed | tf_op | source)
XLA Modules:
  0.0 210.8 jit_solution(11408912797774398587)
XLA Ops:
  6.5 0.0 all-gather.4.cloned.1.call-start
  6.5 0.7 all-gather.4.cloned.1.call-update
  7.3 2.4 %copy.29.down_ref = bf16[4096,64]{1,0:T(8,128)(2,1)} copy(bf16[4096,64]{0,1:T(8,128)(2,1)} %param.8) | data formatting | bytes 1048576 | tf_op args[2]
  9.6 1.0 fusion
  10.6 1.0 pad_maximum_fusion
  11.7 32.9 %all-gather.4.cloned.1.call-done.x_ref = bf16[512,4096]{1,0:T(8,128)(2,1)} async-done(((bf16[128,4096]{1,0:T(8,128)(2,1)}), bf16[512,4096]{1,0:T(8,128)(2,1)}) %all-gather.4.cloned.1.call-update) | async-done | bytes 4194320 | tf_op jit(solution)/shard_map/all_gather | solution.py:222
  44.5 14.5 %project.1 = bf16[4,12,128,128]{3,2,1,0:T(8,128)(2,1)} custom-call(bf16[512,4096]{1,0:T(8,128)(2,1)} %all-gather.4.cloned.1.call-done.x_ref, bf16[4096,1536]{1,0:T(8,128)(2,1)} %w_ref.1, bf16[4096,64]{1,0:T(8,128)(2,1)} %copy.29.down_ref, bf16[64,1536]{1,0:T(8,128)(2,1)} %up_ref.1, f32[512,128]{1,0:T(8,128)} %get-tuple-element.10.cos_ref, ...), custom_call_target="tpu_custom_call" | custom-call | tf_op jit(solution)/shard_map/project/pallas_call | solution.py:66
  59.0 0.0 copy-start.4
  59.0 3.7 %all-to-all-start = ((bf16[4,12,128,128]{3,2,1,0:T(8,128)(2,1)}), bf16[4,12,128,128]{3,2,1,0:T(8,128)(2,1)S(1)}, u32[]{:S(2)}, u32[]{:S(2)}) async-start(bf16[4,12,128,128]{3,2,1,0:T(8,128)(2,1)} %project.1), calls=%async_computation | async-start | bytes 3145728 | tf_op jit(solution)/shard_map/all_to_all | solution.py:227
  62.7 0.0 all-gather.6.cloned.1.call-start
  62.8 0.0 copy-done.4
  62.8 0.2 convert_reduce_fusion
  63.0 0.0 copy-start.3
  63.0 0.1 select_reduce_fusion
  63.1 0.1 reduce_sum.22
  63.2 0.1 pad_add_fusion
  63.3 0.6 reshape.187.index_ref
  63.9 18.8 %all-to-all-done = bf16[4,12,128,128]{3,2,1,0:T(8,128)(2,1)S(1)} async-done(((bf16[4,12,128,128]{3,2,1,0:T(8,128)(2,1)}), bf16[4,12,128,128]{3,2,1,0:T(8,128)(2,1)S(1)}, u32[]{:S(2)}, u32[]{:S(2)}) %all-to-all-start) | async-done | bytes 1572896 | tf_op jit(solution)/shard_map/all_to_all | solution.py:227
  82.7 0.0 copy-start.1
  82.7 1.2 copy-done.1
  83.9 2.9 %select_heads.1 = bf16[48,128,128]{2,1,0:T(8,128)(2,1)} custom-call(s32[48]{0:T(128)} %reshape.187.index_ref, bf16[48,128,128]{2,1,0:T(8,128)(2,1)} %bitcast.12), custom_call_target="tpu_custom_call" | custom-call | tf_op jit(solution)/shard_map/select_heads/pallas_call | solution.py:91
  86.8 0.0 copy-done.3
  86.8 40.6 %all_to_all.15.q_ref = bf16[8,6,128,128]{3,2,1,0:T(8,128)(2,1)S(1)} all-to-all(bf16[8,6,128,128]{3,2,1,0:T(8,128)(2,1)} %bitcast.13), channel_id=1, replica_groups=mesh['seq'=8,'tp'=4] {'seq'}, dimensions={0} | all-to-all | bytes 3145728 | tf_op jit(solution)/shard_map/all_to_all | solution.py:229
  127.4 0.0 copy-start
  127.4 0.0 copy-start.2
  127.4 0.9 slice.27
  128.3 0.0 all-gather.6.cloned.1.call-update
  128.3 0.0 copy-done.2
  128.3 0.1 slice_compare_fusion
  128.4 0.1 add_select_fusion
  128.4 0.3 reduce-window.9
  128.7 0.1 slice.25
  128.8 0.1 reduce-window.12
  128.9 0.1 slice_reduce_fusion
  129.0 0.1 reshape.185
  129.1 0.1 copy.27
  129.2 0.1 copy_maximum_fusion
  129.2 1.0 copy.30.begin_ref
  130.3 0.5 multiply_add_fusion.place_ref
  130.8 0.1 fusion.18
  130.9 0.6 slice_reduce_fusion.1.first_ref
  131.6 19.4 %all-gather.6.cloned.1.call-done = bf16[32,2,128,128]{3,2,1,0:T(8,128)(2,1)} async-done(((bf16[8,2,128,128]{3,2,1,0:T(8,128)(2,1)}), bf16[32,2,128,128]{3,2,1,0:T(8,128)(2,1)}) %all-gather.6.cloned.1.call-update) | async-done | bytes 2097168 | tf_op jit(solution)/shard_map/all_gather | solution.py:230
  151.0 0.0 copy-done
  151.0 20.9 %attend.1 = bf16[8,4,128,128]{3,2,1,0:T(8,128)(2,1)} custom-call(s32[8]{0:T(128)} %slice_reduce_fusion.1.first_ref, s32[8]{0:T(128)} %multiply_add_fusion.place_ref, bf16[8,6,128,128]{3,2,1,0:T(8,128)(2,1)} %copy-done, bf16[4,8,2,128,128]{4,3,2,1,0:T(8,128)(2,1)} %bitcast.15, s32[1024,1]{1,0:T(8,128)} %copy.30.begin_ref), custom_call_target="tpu_custom_call" | custom-call | tf_op jit(solution)/shard_map/attend/pallas_call | solution.py:159
  171.8 29.7 %all_to_all.16 = bf16[8,4,128,128]{3,2,1,0:T(8,128)(2,1)} all-to-all(bf16[8,4,128,128]{3,2,1,0:T(8,128)(2,1)} %attend.1), channel_id=1, replica_groups=mesh['seq'=8,'tp'=4] {'seq'}, dimensions={0} | all-to-all | bytes 2097152 | tf_op jit(solution)/shard_map/all_to_all | solution.py:234
  201.5 2.5 %merge_heads.1 = bf16[128,4096]{1,0:T(8,128)(2,1)} custom-call(s32[32]{0:T(128)} %copy-done.3, bf16[32,128,128]{2,1,0:T(8,128)(2,1)} %bitcast.14), custom_call_target="tpu_custom_call" | custom-call | tf_op jit(solution)/shard_map/merge_heads/pallas_call | solution.py:107
  (7 shorter events, 0.1 us)
Async XLA Ops:
  6.5 38.0 %all-gather.4.cloned.1.call-start = ((), (), s32[]{:S(2)}) async-start(), calls=%async_computation.3 | async-start | bytes 5242880 | tf_op jit(solution)/shard_map/all_gather | solution.py:222
  59.0 3.8 %copy-start.4 = (s32[32]{0:T(128)S(1)}, s32[32]{0:T(128)}, u32[]{:S(2)}) copy-start(s32[32]{0:T(128)} %param.11) | copy-start | bytes 388
  59.0 23.7 %all-to-all-start = ((bf16[4,12,128,128]{3,2,1,0:T(8,128)(2,1)}), bf16[4,12,128,128]{3,2,1,0:T(8,128)(2,1)S(1)}, u32[]{:S(2)}, u32[]{:S(2)}) async-start(bf16[4,12,128,128]{3,2,1,0:T(8,128)(2,1)} %project.1), calls=%async_computation | async-start | bytes 3145728 | tf_op jit(solution)/shard_map/all_to_all | solution.py:227
  62.7 88.2 %all-gather.6.cloned.1.call-start = ((), (), s32[]{:S(2)}) async-start(), calls=%async_computation.4 | async-start | bytes 2621440 | tf_op jit(solution)/shard_map/all_gather | solution.py:230
  63.0 23.8 %copy-start.3 = (s32[32]{0:T(128)}, s32[32]{0:T(128)S(1)}, u32[]{:S(2)}) copy-start(s32[32]{0:T(128)S(1)} %multiply_add_fusion.1.index_ref) | copy-start | bytes 388
  82.7 1.2 copy-start.1
  127.4 23.6 %copy-start = (bf16[8,6,128,128]{3,2,1,0:T(8,128)(2,1)}, bf16[8,6,128,128]{3,2,1,0:T(8,128)(2,1)S(1)}, u32[]{:S(2)}) copy-start(bf16[8,6,128,128]{3,2,1,0:T(8,128)(2,1)S(1)} %all_to_all.15.q_ref) | copy-start | bytes 4718596
  127.4 0.9 copy-start.2
Sparse Core Ops, SparseCore 0:
  8.9 35.5 all-gather.3
  128.4 22.5 all-gather.5

commit v2 on v1

--- a/solution.py
+++ b/solution.py
@@ -26,75 +26,224 @@
     return jnp.concatenate([cosine, cosine], 1), jnp.concatenate([-sine, sine], 1)
 
 
-def project_kernel(rotated_pairs, x_ref, w_ref, down_ref, up_ref, cos_ref, sin_ref, out_ref, mid_ref):
-    step = pl.program_id(0)
-    chunks, pair, rows, _ = out_ref.shape
-
-    @pl.when(step == 0)
-    def _():
-        mid_ref[...] = jnp.dot(
-            x_ref[...], down_ref[...], preferred_element_type=jnp.float32
+MESH = pl.DeviceIdType.MESH
+
+
+def front_kernel(
+    rotated_pairs, here, index_ref, tokens_ref, w_ref, down_ref, up_ref, cos_ref, sin_ref,
+    q_ref, kv_ref,
+    x_all, w_all, stage, landed, sent, mid_ref,
+    w_sem, local_sem, send_sem, x_sem, land_sem, q_sem, kv_sem, spread_sem,
+):
+    tp = lax.axis_index("tp")
+    seq = lax.axis_index("seq")
+    chips, _, own, _ = x_all.shape
+    halves, half = 2, own // 2
+    tp_count, seq_count = 2 * chips, q_ref.shape[0]
+    steps = w_all.shape[0]
+    wide = w_all.shape[2]
+    pair = wide // DH
+    chip, core = tp // 2, tp % 2
+    partner = chip * 2 + (1 - core)
+    sends = []
+
+    def send(src, dst, sem, axis, target):
+        copy = pltpu.make_async_remote_copy(
+            src_ref=src, dst_ref=dst, send_sem=send_sem.at[len(sends)], recv_sem=sem,
+            device_id={axis: target}, device_id_type=MESH,
+        )
+        copy.start()
+        sends.append(copy)
+
+    def arrived(dst, sem, axis, source):
+        pltpu.make_async_remote_copy(
+            src_ref=dst, dst_ref=dst, send_sem=send_sem.at[0], recv_sem=sem,
+            device_id={axis: source}, device_id_type=MESH,
+        ).wait_recv()
+
+    def weight_copy(step):
+        return pltpu.make_async_copy(
+            w_ref.at[:, pl.ds(pl.multiple_of(step * wide, wide), wide)], w_all.at[step], w_sem.at[step]
+        )
+
+    own_copy = pltpu.make_async_copy(tokens_ref, x_all.at[chip, core], local_sem.at[0])
+    own_copy.start()
+    for step in range(steps):
+        weight_copy(step).start()
+
+    barrier = pltpu.get_barrier_semaphore()
+    for k in range(1, tp_count):
+        pl.semaphore_signal(
+            barrier, inc=1, device_id={"tp": (tp + k) % tp_count}, device_id_type=MESH
+        )
+    for k in range(1, seq_count):
+        pl.semaphore_signal(
+            barrier, inc=1, device_id={"seq": (seq + k) % seq_count}, device_id_type=MESH
+        )
+    pl.semaphore_wait(barrier, tp_count - 1 + seq_count - 1)
+
+    def rows_of(h):
+        return pl.ds(h * half, half)
+
+    others = [(chip + k) % chips for k in range(1, chips)]
+    for h in range(halves):
+        for other in others:
+            send(
+                tokens_ref.at[rows_of(h)], x_all.at[chip, core, rows_of(h)],
+                x_sem.at[chip, core, h], "tp", other * 2 + core,
+            )
+        send(
+            tokens_ref.at[rows_of(h)], x_all.at[chip, core, rows_of(h)],
+            x_sem.at[chip, core, h], "tp", partner,
+        )
+
+    def compute(where, low, count, first):
+        rows = pl.ds(low, count)
+        x = x_all[where, :, rows, :].reshape(2 * count, x_all.shape[3])
+        mid_ref[pl.ds(0, 2 * count)] = jnp.dot(
+            x, down_ref[...], preferred_element_type=jnp.float32
         ).astype(jnp.bfloat16)
 
-    joined = jnp.dot(x_ref[...], w_ref[...], preferred_element_type=jnp.float32)
-    joined = joined + ADAPTER_SCALE * jnp.dot(
-        mid_ref[...], up_ref[...], preferred_element_type=jnp.float32
-    )
-
-    def store(head, value):
-        value = value.astype(jnp.bfloat16)
-        for chunk in range(chunks):
-            out_ref[chunk, head] = value[chunk * rows : (chunk + 1) * rows]
-
-    @pl.when(step < rotated_pairs)
-    def _():
-        for head in range(pair):
-            part = joined[:, head * DH : (head + 1) * DH]
-            store(head, part * cos_ref[...] + pltpu.roll(part, DH // 2, 1) * sin_ref[...])
-
-    @pl.when(step >= rotated_pairs)
-    def _():
-        for head in range(pair):
-            store(head, joined[:, head * DH : (head + 1) * DH])
-
-
-def project(x, w, down, up, cosine, sine, tp_count, rotated_heads):
-    rows, width = x.shape
+        @pl.loop(0, steps)
+        def _(step):
+            if first:
+                weight_copy(step).wait()
+            x = x_all[where, :, rows, :].reshape(2 * count, x_all.shape[3])
+            joined = jnp.dot(x, w_all[step], preferred_element_type=jnp.float32)
+            joined = joined + ADAPTER_SCALE * jnp.dot(
+                mid_ref[pl.ds(0, 2 * count)], up_ref[step], preferred_element_type=jnp.float32
+            )
+            kind = step // rotated_pairs
+            cosine = cos_ref[kind, where, :, rows, :].reshape(2 * count, DH)
+            sine = sin_ref[kind, where, :, rows, :].reshape(2 * count, DH)
+            for head in range(pair):
+                part = joined[:, head * DH : (head + 1) * DH]
+                part = part * cosine + pltpu.roll(part, DH // 2, 1) * sine
+                part = part.astype(jnp.bfloat16)
+                for k in range(2):
+                    stage[where, k, step * pair + head, rows] = part[k * count : (k + 1) * count]
+
+    def give(where, k, h, target):
+        send(
+            stage.at[where, k, :, rows_of(h)], landed.at[tp, :, rows_of(h)],
+            land_sem.at[tp, h], "tp", target,
+        )
+
+    own_copy.wait()
+    for h in range(halves):
+        arrived(x_all.at[chip, 1 - core, rows_of(h)], x_sem.at[chip, 1 - core, h], "tp", partner)
+    compute(chip, 0, own, True)
+    keep = pltpu.make_async_copy(stage.at[chip, core], landed.at[tp], local_sem.at[0])
+    keep.start()
+    for h in range(halves):
+        give(chip, 1 - core, h, partner)
+    for h in range(halves):
+        for other in others:
+            block = x_all.at[other, core, rows_of(h)]
+            arrived(block, x_sem.at[other, core, h], "tp", other * 2 + core)
+            send(block, block, x_sem.at[other, core, h], "tp", partner)
+        for other in others:
+            arrived(
+                x_all.at[other, 1 - core, rows_of(h)], x_sem.at[other, 1 - core, h], "tp", partner
+            )
+            compute(other, h * half, half, False)
+            for k in range(2):
+                give(other, k, h, other * 2 + k)
+    keep.wait()
+    for k in range(1, tp_count):
+        source = (tp + k) % tp_count
+        for h in range(halves):
+            arrived(landed.at[source, :, rows_of(h)], land_sem.at[source, h], "tp", source)
+
+    local = landed.shape[1]
+    slabs = here + 2
+
+    def pick(slot):
+        flat = index_ref[slot]
+        sent[slot // slabs, slot % slabs] = landed[flat // local, flat % local]
+
+    @pl.loop(0, seq_count)
+    def _(j):
+        for slot in range(here, slabs):
+            pick(j * slabs + slot)
+
+    near = [(seq + k) % seq_count for k in range(1, seq_count)]
+    for j in near:
+        send(sent.at[j, pl.ds(here, 2)], kv_ref.at[tp, seq], kv_sem.at[seq], "seq", j)
+
+    @pl.loop(0, seq_count)
+    def _(j):
+        for slot in range(here):
+            pick(j * slabs + slot)
+
+    for j in near:
+        send(sent.at[j, pl.ds(0, here)], q_ref.at[seq], q_sem.at[seq], "seq", j)
+    mine_kv = pltpu.make_async_copy(
+        sent.at[seq, pl.ds(here, 2)], kv_ref.at[tp, seq], local_sem.at[0]
+    )
+    mine_q = pltpu.make_async_copy(sent.at[seq, pl.ds(0, here)], q_ref.at[seq], local_sem.at[1])
+    mine_kv.start()
+    mine_q.start()
+    mine_kv.wait()
+    for n, source in enumerate([seq] + near[::-1]):
+        block = kv_ref.at[tp, source]
+        if n:
+            arrived(block, kv_sem.at[source], "seq", source)
+        for k in range(1, tp_count):
+            send(block, block, spread_sem.at[tp, source], "tp", (tp + k) % tp_count)
+    mine_q.wait()
+    for source in near:
+        arrived(q_ref.at[source], q_sem.at[source], "seq", source)
+    for k in range(1, tp_count):
+        source = (tp + k) % tp_count
+        for s in range(seq_count):
+            arrived(kv_ref.at[source, s], spread_sem.at[source, s], "tp", source)
+    for copy in sends:
+        copy.wait_send()
+
+
+def front(index, tokens, w, down, up, cosine, sine, tp_count, seq_count, rotated_heads):
+    own, width = tokens.shape
     heads = w.shape[1] // DH
     pair = 2
-    own = rows // tp_count
+    steps = heads // pair
+    chips = tp_count // 2
+    here = H // seq_count
+    rank = down.shape[1]
+    up = up.reshape(rank, steps, pair * DH).transpose(1, 0, 2)
+    vmem = pl.BlockSpec(memory_space=pltpu.VMEM)
+    anywhere = pl.BlockSpec(memory_space=pl.ANY)
+    count = (
+        2 * chips + 2 + 2 * (chips - 1) * 3 + 2 * (seq_count - 1) + seq_count * (tp_count - 1)
+    )
+    bf16 = jnp.bfloat16
     return pl.pallas_call(
-        functools.partial(project_kernel, rotated_heads // pair),
-        grid=(heads // pair,),
-        in_specs=[
-            pl.BlockSpec((rows, width), lambda i: (0, 0)),
-            pl.BlockSpec((width, pair * DH), lambda i: (0, i)),
-            pl.BlockSpec(down.shape, lambda i: (0, 0)),
-            pl.BlockSpec((up.shape[0], pair * DH), lambda i: (0, i)),
-            pl.BlockSpec((rows, DH), lambda i: (0, 0)),
-            pl.BlockSpec((rows, DH), lambda i: (0, 0)),
+        functools.partial(front_kernel, rotated_heads // pair, here),
+        in_specs=[pl.BlockSpec(memory_space=pltpu.SMEM), anywhere, anywhere, vmem, vmem, vmem, vmem],
+        out_specs=[anywhere, anywhere],
+        out_shape=[
+            jax.ShapeDtypeStruct((seq_count, here, own, DH), bf16),
+            jax.ShapeDtypeStruct((tp_count, seq_count, 2, own, DH), bf16),
         ],
-        out_specs=pl.BlockSpec((tp_count, pair, own, DH), lambda i: (0, i, 0, 0)),
-        out_shape=jax.ShapeDtypeStruct((tp_count, heads, own, DH), jnp.bfloat16),
-        scratch_shapes=[pltpu.VMEM((rows, down.shape[1]), jnp.bfloat16)],
-        name="project",
-    )(x, w, down, up, cosine, sine)
-
-
-def select_kernel(index_ref, in_ref, out_ref):
-    @pl.loop(0, out_ref.shape[0])
-    def _(slot):
-        out_ref[slot] = in_ref[index_ref[slot]]
-
-
-def select(index, slabs):
-    return pl.pallas_call(
-        select_kernel,
-        in_specs=[pl.BlockSpec(memory_space=pltpu.SMEM), pl.BlockSpec(memory_space=pltpu.VMEM)],
-        out_specs=pl.BlockSpec(memory_space=pltpu.VMEM),
-        out_shape=jax.ShapeDtypeStruct((index.shape[0],) + slabs.shape[1:], slabs.dtype),
-        name="select_heads",
-    )(index, slabs)
+        scratch_shapes=[
+            pltpu.VMEM((chips, 2, own, width), bf16),
+            pltpu.VMEM((steps, width, pair * DH), bf16),
+            pltpu.VMEM((chips, 2, heads, own, DH), bf16),
+            pltpu.VMEM((tp_count, heads, own, DH), bf16),
+            pltpu.VMEM((seq_count, here + 2, own, DH), bf16),
+            pltpu.VMEM((2 * own, rank), bf16),
+            pltpu.SemaphoreType.DMA((steps,)),
+            pltpu.SemaphoreType.DMA((2,)),
+            pltpu.SemaphoreType.DMA((count,)),
+            pltpu.SemaphoreType.DMA((chips, 2, 2)),
+            pltpu.SemaphoreType.DMA((tp_count, 2)),
+            pltpu.SemaphoreType.DMA((seq_count,)),
+            pltpu.SemaphoreType.DMA((seq_count,)),
+            pltpu.SemaphoreType.DMA((tp_count, seq_count)),
+        ],
+        compiler_params=pltpu.CompilerParams(collective_id=0, has_side_effects=True),
+        name="front",
+    )(index, tokens, w, down, up, cosine, sine)
 
 
 def merge_kernel(index_ref, in_ref, out_ref):
@@ -219,15 +368,13 @@
         begin.reshape(seq_count, tp_count, own), tp_rank, 1, 1
     ).reshape(seq_count, own)
 
-    rows = lax.all_gather(tokens, "tp", axis=0, tiled=True)
-    heads = project(
-        rows, joined_projection_weight, adapter_down_weight, adapter_up_weight,
-        cosine, sine, tp_count, q_per + kv_per,
-    )
-    heads = lax.all_to_all(heads, "tp", split_axis=0, concat_axis=0, tiled=True)
-    sent = select(index, heads.reshape(-1, own, DH)).reshape(seq_count, here + 2, own, DH)
-    held = lax.all_to_all(sent, "seq", split_axis=0, concat_axis=0, tiled=True)
-    kv = lax.all_gather(held[:, here:], "tp", axis=0)
+    table = (1, tp_count // 2, 2, own, DH)
+    cosine = jnp.concatenate([cosine.reshape(table), jnp.ones(table, jnp.float32)])
+    sine = jnp.concatenate([sine.reshape(table), jnp.zeros(table, jnp.float32)])
+    held, kv = front(
+        index, tokens, joined_projection_weight, adapter_down_weight, adapter_up_weight,
+        cosine, sine, tp_count, seq_count, q_per + kv_per,
+    )
     context = attend(
         begin[:, 0], first_place, held, kv, begin.reshape(seq_count * own, 1), here
     )

time: 214 us -> 144 us (0.67)
  the two profiles are of different devices: /device:TPU:10 before, /device:TPU:0 now
where the time goes in v2:
time: 144 us; the launch traced here: 143 us
  Pallas kernels  92.7 us (64%)
  blocking collectives  37.8 us (26%)
  local copies, waits for them, and re-layouts  6.82 us (5%)
  other arithmetic  5.95 us (4%)
    pallas_call x1, Pallas kernels, front(): pl.pallas_call(functools.partial(front_kernel, rotated_heads // pair, her...  74.2 us
    all_to_all x1, blocking collectives, per_device(): lax.all_to_all(context, 'seq', split_axis=0, concat_axis=0, tiled=True)  37.8 us
    pallas_call x1, Pallas kernels, attend(): pl.pallas_call(functools.partial(attend_kernel, heads), grid_spec=pltpu.P...  16 us

profile of v2, /device:TPU:0, one launch (start us, length us, event | category | flops | bytes accessed | tf_op | source)
XLA Modules:
  0.0 143.3 jit_solution(7462265280563759325)
XLA Ops:
  0.0 0.9 slice_compare_fusion
  0.9 0.1 add_select_fusion
  1.0 0.3 reduce-window.9
  1.3 0.1 slice.21
  1.3 0.1 reduce-window.12
  1.4 0.1 slice_reduce_fusion
  1.5 0.1 reshape.248
  1.6 0.1 copy.26
  1.7 0.1 fusion.18
  1.8 0.1 copy_maximum_fusion
  1.9 0.9 convert_reduce_fusion
  2.8 0.7 multiply_add_fusion.1.index_ref
  3.4 0.0 copy-start
  3.4 0.7 slice_reduce_fusion.1.first_ref
  4.1 0.5 multiply_add_fusion.place_ref
  4.7 0.1 select_reduce_fusion
  4.8 0.1 reduce_sum.22
  4.9 0.1 pad_add_fusion
  5.0 0.7 reshape.250.index_ref
  5.6 2.4 %copy.29.down_ref = bf16[4096,64]{1,0:T(8,128)(2,1)} copy(bf16[4096,64]{0,1:T(8,128)(2,1)} %param.8) | data formatting | bytes 1048576 | tf_op args[2]
  8.0 1.6 %copy.37 = bf16[8,6,8,256]{3,2,0,1:T(8,128)(2,1)} copy(bf16[8,6,8,256]{3,2,1,0:T(8,128)(2,1)} %bitcast.18) | data formatting | bytes 393216 | tf_op jit(solution)/shard_map/reshape | solution.py:213
  9.6 1.0 copy.30.begin_ref
  10.6 1.0 fusion
  11.6 1.2 select_maximum_fusion
  12.8 74.2 %front.1 = (bf16[8,4,128,128]{3,2,1,0:T(8,128)(2,1)}, bf16[4,8,2,128,128]{4,3,2,1,0:T(8,128)(2,1)}) custom-call(s32[48]{0:T(128)} %reshape.250.index_ref, bf16[128,4096]{1,0:T(8,128)(2,1)} %tokens_ref.1, bf16[4096,1536]{1,0:T(8,128)(2,1)} %w_ref.1, bf16[4096,64]{1,0:T(8,128)(2,1)} %copy.29.down_ref, bf16[6,64,256]{2,1,0:T(8,128)(2,1)} %bitcast.17, ...), custom_call_target="tpu_custom_call" | custom-call | tf_op jit(solution)/shard_map/front/pallas_call | solution.py:220
  87.0 16.0 %attend.1 = bf16[8,4,128,128]{3,2,1,0:T(8,128)(2,1)} custom-call(s32[8]{0:T(128)} %slice_reduce_fusion.1.first_ref, s32[8]{0:T(128)} %multiply_add_fusion.place_ref, bf16[8,4,128,128]{3,2,1,0:T(8,128)(2,1)} %get-tuple-element.7.q_ref, bf16[4,8,2,128,128]{4,3,2,1,0:T(8,128)(2,1)} %get-tuple-element.8.kv_ref, s32[1024,1]{1,0:T(8,128)} %copy.30.begin_ref), custom_call_target="tpu_custom_call" | custom-call | tf_op jit(solution)/shard_map/attend/pallas_call | solution.py:308
  103.0 0.0 copy-done
  103.0 37.8 %all_to_all.5 = bf16[8,4,128,128]{3,2,1,0:T(8,128)(2,1)} all-to-all(bf16[8,4,128,128]{3,2,1,0:T(8,128)(2,1)} %attend.1), channel_id=1, replica_groups=mesh['seq'=8,'tp'=4] {'seq'}, dimensions={0} | all-to-all | bytes 2097152 | tf_op jit(solution)/shard_map/all_to_all | solution.py:381
  140.8 2.5 %merge_heads.1 = bf16[128,4096]{1,0:T(8,128)(2,1)} custom-call(s32[32]{0:T(128)} %copy-done, bf16[32,128,128]{2,1,0:T(8,128)(2,1)} %bitcast.16), custom_call_target="tpu_custom_call" | custom-call | tf_op jit(solution)/shard_map/merge_heads/pallas_call | solution.py:256
  (6 shorter events, 0.1 us)
Async XLA Ops:
  3.4 99.6 %copy-start = (s32[32]{0:T(128)}, s32[32]{0:T(128)S(1)}, u32[]{:S(2)}) copy-start(s32[32]{0:T(128)S(1)} %multiply_add_fusion.1.index_ref) | copy-start | bytes 388

commit v3 on v2

--- a/solution.py
+++ b/solution.py
@@ -100,8 +100,8 @@
     def compute(where, low, count, first):
         rows = pl.ds(low, count)
         x = x_all[where, :, rows, :].reshape(2 * count, x_all.shape[3])
-        mid_ref[pl.ds(0, 2 * count)] = jnp.dot(
-            x, down_ref[...], preferred_element_type=jnp.float32
+        mid_ref[pl.ds(0, 2 * count)] = lax.dot_general(
+            x, down_ref[...], (((1,), (1,)), ((), ())), preferred_element_type=jnp.float32
         ).astype(jnp.bfloat16)
 
         @pl.loop(0, steps)
@@ -111,7 +111,8 @@
             x = x_all[where, :, rows, :].reshape(2 * count, x_all.shape[3])
             joined = jnp.dot(x, w_all[step], preferred_element_type=jnp.float32)
             joined = joined + ADAPTER_SCALE * jnp.dot(
-                mid_ref[pl.ds(0, 2 * count)], up_ref[step], preferred_element_type=jnp.float32
+                mid_ref[pl.ds(0, 2 * count)], up_ref[:, pl.ds(pl.multiple_of(step * wide, wide), wide)],
+                preferred_element_type=jnp.float32
             )
             kind = step // rotated_pairs
             cosine = cos_ref[kind, where, :, rows, :].reshape(2 * count, DH)
@@ -155,17 +156,16 @@
         for h in range(halves):
             arrived(landed.at[source, :, rows_of(h)], land_sem.at[source, h], "tp", source)
 
-    local = landed.shape[1]
-    slabs = here + 2
-
-    def pick(slot):
-        flat = index_ref[slot]
-        sent[slot // slabs, slot % slabs] = landed[flat // local, flat % local]
+    q_per = H // tp_count
+    kv_per = KV // tp_count
 
     @pl.loop(0, seq_count)
     def _(j):
-        for slot in range(here, slabs):
-            pick(j * slabs + slot)
+        kv_head = j * here // GROUP
+        for k in range(2):
+            sent[j, here + k] = landed[
+                kv_head // kv_per, q_per + k * kv_per + kv_head % kv_per
+            ]
 
     near = [(seq + k) % seq_count for k in range(1, seq_count)]
     for j in near:
@@ -173,8 +173,9 @@
 
     @pl.loop(0, seq_count)
     def _(j):
-        for slot in range(here):
-            pick(j * slabs + slot)
+        for k in range(here):
+            head = index_ref[j * here + k]
+            sent[j, k] = landed[head // q_per, head % q_per]
 
     for j in near:
         send(sent.at[j, pl.ds(0, here)], q_ref.at[seq], q_sem.at[seq], "seq", j)
@@ -210,7 +211,6 @@
     chips = tp_count // 2
     here = H // seq_count
     rank = down.shape[1]
-    up = up.reshape(rank, steps, pair * DH).transpose(1, 0, 2)
     vmem = pl.BlockSpec(memory_space=pltpu.VMEM)
     anywhere = pl.BlockSpec(memory_space=pl.ANY)
     count = (
@@ -243,33 +243,70 @@
         ],
         compiler_params=pltpu.CompilerParams(collective_id=0, has_side_effects=True),
         name="front",
-    )(index, tokens, w, down, up, cosine, sine)
-
-
-def merge_kernel(index_ref, in_ref, out_ref):
-    for head in range(in_ref.shape[0]):
-        out_ref[:, head * DH : (head + 1) * DH] = in_ref[index_ref[head]]
-
-
-def merge(index, slabs):
-    heads, rows, _ = slabs.shape
+    )(index, tokens, w, down.T, up, cosine, sine)
+
+
+def finish_kernel(slot_ref, in_ref, out_ref, landed, send_sem, land_sem, local_sem):
+    seq = lax.axis_index("seq")
+    seq_count, here, _, _ = landed.shape
+    own_copy = pltpu.make_async_copy(in_ref.at[seq], landed.at[seq], local_sem.at[0])
+    own_copy.start()
+    near = [(seq + k) % seq_count for k in range(1, seq_count)]
+    barrier = pltpu.get_barrier_semaphore()
+    for j in near:
+        pl.semaphore_signal(barrier, inc=1, device_id={"seq": j}, device_id_type=MESH)
+    pl.semaphore_wait(barrier, seq_count - 1)
+    sends = []
+    for n, j in enumerate(near):
+        copy = pltpu.make_async_remote_copy(
+            src_ref=in_ref.at[j], dst_ref=landed.at[seq], send_sem=send_sem.at[n],
+            recv_sem=land_sem.at[seq], device_id={"seq": j}, device_id_type=MESH,
+        )
+        copy.start()
+        sends.append(copy)
+    own_copy.wait()
+    for j in near:
+        pltpu.make_async_remote_copy(
+            src_ref=landed.at[j], dst_ref=landed.at[j], send_sem=send_sem.at[0],
+            recv_sem=land_sem.at[j], device_id={"seq": j}, device_id_type=MESH,
+        ).wait_recv()
+    for head in range(seq_count * here):
+        slot = slot_ref[head]
+        out_ref[:, head * DH : (head + 1) * DH] = landed[slot // here, slot % here]
+    for copy in sends:
+        copy.wait_send()
+
+
+def finish(slot, context):
+    seq_count, here, rows, _ = context.shape
     return pl.pallas_call(
-        merge_kernel,
-        in_specs=[pl.BlockSpec(memory_space=pltpu.SMEM), pl.BlockSpec(memory_space=pltpu.VMEM)],
+        finish_kernel,
+        in_specs=[pl.BlockSpec(memory_space=pltpu.SMEM), pl.BlockSpec(memory_space=pl.ANY)],
         out_specs=pl.BlockSpec(memory_space=pltpu.VMEM),
-        out_shape=jax.ShapeDtypeStruct((rows, heads * DH), slabs.dtype),
-        name="merge_heads",
-    )(index, slabs)
-
-
-def attend_kernel(heads, first_ref, place_ref, q_ref, kv_ref, begin_ref, out_ref):
+        out_shape=jax.ShapeDtypeStruct((rows, seq_count * here * DH), context.dtype),
+        scratch_shapes=[
+            pltpu.VMEM(context.shape, context.dtype),
+            pltpu.SemaphoreType.DMA((seq_count,)),
+            pltpu.SemaphoreType.DMA((seq_count,)),
+            pltpu.SemaphoreType.DMA((1,)),
+        ],
+        compiler_params=pltpu.CompilerParams(collective_id=1, has_side_effects=True),
+        name="finish",
+    )(slot, context)
+
+
+def attend_kernel(heads, scalar_ref, q_ref, kv_ref, doc_ref, out_ref):
     step = pl.program_id(0)
+    tp = lax.axis_index("tp")
     chunks, _, _, own, _ = kv_ref.shape
     block = chunks * own
     rows = heads * own
     q = q_ref[0, :heads].reshape(rows, DH)
-    place = place_ref[step]
-    begins = jnp.concatenate([begin_ref[...]] * heads, 0)
+    place = step * block + tp * own
+    first = jnp.sum((doc_ref[...] < scalar_ref[place]).astype(jnp.int32))
+    docs = doc_ref[pl.ds(step * chunks + tp, 1), :]
+    docs = jnp.broadcast_to(docs, (own, own)).T[:, :1]
+    docs = jnp.concatenate([docs] * heads, 0)
     places = place + lax.broadcasted_iota(jnp.int32, (own, 1), 0)
     places = jnp.concatenate([places] * heads, 0)
     factor = (DH**-0.5) * LOG2_E
@@ -282,7 +319,10 @@
             q, keys, (((1,), (1,)), ((), ())), preferred_element_type=jnp.float32
         )
         at = index * block + lax.broadcasted_iota(jnp.int32, (1, block), 1)
-        scores = jnp.where((at <= places) & (at >= begins), scores, NEG_BIG)
+        key_docs = jnp.concatenate(
+            [doc_ref[pl.ds(index * chunks + c, 1), :] for c in range(chunks)], 1
+        )
+        scores = jnp.where((at <= places) & (key_docs == docs), scores, NEG_BIG)
         new_top = jnp.maximum(top, jnp.max(scores, 1, keepdims=True))
         shrink = jnp.exp2((top - new_top) * factor)
         powers = jnp.exp2((scores - new_top) * factor)
@@ -299,43 +339,36 @@
         jnp.zeros((rows, DH), jnp.float32),
     )
     carry = body(last, start)
-    top, total, acc = lax.fori_loop(first_ref[step] // block, last, body, carry)
+    top, total, acc = lax.fori_loop(first // block, last, body, carry)
     out_ref[0] = (acc / total).astype(jnp.bfloat16).reshape(heads, own, DH)
 
 
-def attend(first, place, q, kv, begins, heads):
+def attend(document_index, q, kv, heads):
     steps, slabs, own, _ = q.shape
     return pl.pallas_call(
         functools.partial(attend_kernel, heads),
         grid_spec=pltpu.PrefetchScalarGridSpec(
-            num_scalar_prefetch=2,
+            num_scalar_prefetch=1,
             grid=(steps,),
             in_specs=[
                 pl.BlockSpec((1, slabs, own, DH), lambda i, *_: (i, 0, 0, 0)),
                 pl.BlockSpec(kv.shape, lambda i, *_: (0,) * 5),
-                pl.BlockSpec((own, 1), lambda i, *_: (i, 0)),
+                pl.BlockSpec((steps * kv.shape[0], own), lambda i, *_: (0, 0)),
             ],
             out_specs=pl.BlockSpec((1, heads, own, DH), lambda i, *_: (i, 0, 0, 0)),
         ),
         out_shape=jax.ShapeDtypeStruct((steps, heads, own, DH), jnp.bfloat16),
         name="attend",
-    )(first, place, q, kv, begins)
-
-
-def head_tables(query_to_key_head, tp_count, seq_count):
+    )(document_index, q, kv, document_index.reshape(-1, own))
+
+
+def head_tables(query_to_key_head):
     heads = jnp.arange(H, dtype=jnp.int32)
     same = query_to_key_head[:, None] == query_to_key_head[None, :]
     earlier = heads[None, :] < heads[:, None]
     slot = GROUP * query_to_key_head + jnp.sum((same & earlier).astype(jnp.int32), 1)
     order = jnp.sum(jnp.where(slot[None, :] == heads[:, None], heads[None, :], 0), 1)
-    q_per, kv_per = H // tp_count, KV // tp_count
-    local = q_per + 2 * kv_per
-    here = H // seq_count
-    q_index = (order // q_per * local + order % q_per).reshape(seq_count, here)
-    kv_head = jnp.arange(seq_count, dtype=jnp.int32) * here // GROUP
-    k_index = kv_head // kv_per * local + q_per + kv_head % kv_per
-    index = jnp.concatenate([q_index, k_index[:, None], k_index[:, None] + kv_per], 1)
-    return index.reshape(-1).astype(jnp.int32), slot.astype(jnp.int32)
+    return order.astype(jnp.int32), slot.astype(jnp.int32)
 
 
 def per_device(
@@ -355,19 +388,9 @@
     here = H // seq_count
     q_per, kv_per = H // tp_count, KV // tp_count
 
-    index, slot = head_tables(query_to_key_head, tp_count, seq_count)
+    index, slot = head_tables(query_to_key_head)
     places = (seq_rank * block + jnp.arange(block, dtype=jnp.int32)).astype(jnp.float32)
     cosine, sine = rope_tables(places)
-    first_place = jnp.arange(seq_count, dtype=jnp.int32) * block + tp_rank * own
-    all_places = jnp.arange(document_index.shape[0], dtype=jnp.int32)
-    starts_here = jnp.concatenate(
-        [jnp.ones((1,), jnp.bool_), document_index[1:] != document_index[:-1]]
-    )
-    begin = lax.cummax(jnp.where(starts_here, all_places, 0))
-    begin = lax.dynamic_slice_in_dim(
-        begin.reshape(seq_count, tp_count, own), tp_rank, 1, 1
-    ).reshape(seq_count, own)
-
     table = (1, tp_count // 2, 2, own, DH)
     cosine = jnp.concatenate([cosine.reshape(table), jnp.ones(table, jnp.float32)])
     sine = jnp.concatenate([sine.reshape(table), jnp.zeros(table, jnp.float32)])
@@ -375,11 +398,8 @@
         index, tokens, joined_projection_weight, adapter_down_weight, adapter_up_weight,
         cosine, sine, tp_count, seq_count, q_per + kv_per,
     )
-    context = attend(
-        begin[:, 0], first_place, held, kv, begin.reshape(seq_count * own, 1), here
-    )
-    context = lax.all_to_all(context, "seq", split_axis=0, concat_axis=0, tiled=True)
-    return merge(slot, context.reshape(H, own, DH))
+    context = attend(document_index, held, kv, here)
+    return finish(slot, context)
 
 
 def solution(mesh):

time: 144 us -> 135 us (0.938)
  the two profiles are of different devices: /device:TPU:0 before, /device:TPU:10 now
where the time goes in v3:
time: 135 us
  Pallas kernels  128 us (95%)
  other arithmetic  4.47 us (3%)
  local copies, waits for them, and re-layouts  2.29 us (2%)
    pallas_call x1, Pallas kernels, front(): pl.pallas_call(functools.partial(front_kernel, rotated_heads // pair, her...  79.9 us
    pallas_call x1, Pallas kernels, finish(): pl.pallas_call(finish_kernel, in_specs=[pl.BlockSpec(memory_space=pltpu.S...  29.4 us
    pallas_call x1, Pallas kernels, attend(): pl.pallas_call(functools.partial(attend_kernel, heads), grid_spec=pltpu.P...  19.1 us

profile of v3, /device:TPU:10, one launch (start us, length us, event | category | flops | bytes accessed | tf_op | source)
XLA Modules:
  0.0 135.2 jit_solution(10426873383977596769)
XLA Ops:
  0.0 0.9 convert_reduce_fusion
  0.9 0.7 multiply_add_fusion.slot_ref
  1.6 0.0 copy-start
  1.6 0.7 select_reduce_fusion.index_ref
  2.3 1.0 fusion
  3.3 1.2 select_maximum_fusion
  4.5 79.9 %front.1 = (bf16[8,4,128,128]{3,2,1,0:T(8,128)(2,1)}, bf16[4,8,2,128,128]{4,3,2,1,0:T(8,128)(2,1)}) custom-call(s32[32]{0:T(128)} %select_reduce_fusion.index_ref, bf16[128,4096]{1,0:T(8,128)(2,1)} %tokens_ref.1, bf16[4096,1536]{1,0:T(8,128)(2,1)} %w_ref.1, bf16[64,4096]{1,0:T(8,128)(2,1)} %bitcast.2, bf16[64,1536]{1,0:T(8,128)(2,1)} %up_ref.1, ...), custom_call_target="tpu_custom_call" | custom-call | tf_op jit(solution)/shard_map/front/pallas_call | solution.py:220
  84.4 19.1 %attend.1.in_ref = bf16[8,4,128,128]{3,2,1,0:T(8,128)(2,1)} custom-call(s32[4096]{0:T(1024)} %scalar_ref.1, bf16[8,4,128,128]{3,2,1,0:T(8,128)(2,1)} %get-tuple-element.7.q_ref, bf16[4,8,2,128,128]{4,3,2,1,0:T(8,128)(2,1)} %get-tuple-element.8.kv_ref, s32[32,128]{1,0:T(8,128)} %bitcast.3), custom_call_target="tpu_custom_call" | custom-call | tf_op jit(solution)/shard_map/attend/pallas_call | solution.py:348
  103.5 0.0 copy-done
  103.5 29.4 %finish.1 = bf16[128,4096]{1,0:T(8,128)(2,1)} custom-call(s32[32]{0:T(128)} %copy-done, bf16[8,4,128,128]{3,2,1,0:T(8,128)(2,1)} %attend.1.in_ref), custom_call_target="tpu_custom_call" | custom-call | tf_op jit(solution)/shard_map/finish/pallas_call | solution.py:282
  132.9 2.3 %copy.8 = bf16[128,4096]{1,0:T(8,128)(2,1)} copy(bf16[128,4096]{1,0:T(8,128)(2,1)} %finish.1) | data formatting | bytes 2097152
  (2 shorter events, 0.0 us)
Async XLA Ops:
  1.6 101.9 %copy-start = (s32[32]{0:T(128)}, s32[32]{0:T(128)S(1)}, u32[]{:S(2)}) copy-start(s32[32]{0:T(128)S(1)} %multiply_add_fusion.slot_ref) | copy-start | bytes 388

commit v4 on v3

--- a/solution.py
+++ b/solution.py
@@ -32,7 +32,7 @@
 def front_kernel(
     rotated_pairs, here, index_ref, tokens_ref, w_ref, down_ref, up_ref, cos_ref, sin_ref,
     q_ref, kv_ref,
-    x_all, w_all, stage, landed, sent, mid_ref,
+    x_all, w_all, stage, landed_low, landed_high, sent, mid_ref,
     w_sem, local_sem, send_sem, x_sem, land_sem, q_sem, kv_sem, spread_sem,
 ):
     tp = lax.axis_index("tp")
@@ -45,6 +45,7 @@
     pair = wide // DH
     chip, core = tp // 2, tp % 2
     partner = chip * 2 + (1 - core)
+    landed = (landed_low, landed_high)
     sends = []
 
     def send(src, dst, sem, axis, target):
@@ -126,7 +127,7 @@
 
     def give(where, k, h, target):
         send(
-            stage.at[where, k, :, rows_of(h)], landed.at[tp, :, rows_of(h)],
+            stage.at[where, k, :, rows_of(h)], landed[h].at[tp],
             land_sem.at[tp, h], "tp", target,
         )
 
@@ -134,8 +135,14 @@
     for h in range(halves):
         arrived(x_all.at[chip, 1 - core, rows_of(h)], x_sem.at[chip, 1 - core, h], "tp", partner)
     compute(chip, 0, own, True)
-    keep = pltpu.make_async_copy(stage.at[chip, core], landed.at[tp], local_sem.at[0])
-    keep.start()
+    keeps = [
+        pltpu.make_async_copy(
+            stage.at[chip, core, :, rows_of(h)], landed[h].at[tp], local_sem.at[5 * h]
+        )
+        for h in range(halves)
+    ]
+    for keep in keeps:
+        keep.start()
     for h in range(halves):
         give(chip, 1 - core, h, partner)
     for h in range(halves):
@@ -150,55 +157,70 @@
             compute(other, h * half, half, False)
             for k in range(2):
                 give(other, k, h, other * 2 + k)
-    keep.wait()
-    for k in range(1, tp_count):
-        source = (tp + k) % tp_count
-        for h in range(halves):
-            arrived(landed.at[source, :, rows_of(h)], land_sem.at[source, h], "tp", source)
-
+    for keep in keeps:
+        keep.wait()
     q_per = H // tp_count
     kv_per = KV // tp_count
-
-    @pl.loop(0, seq_count)
-    def _(j):
-        kv_head = j * here // GROUP
-        for k in range(2):
-            sent[j, here + k] = landed[
-                kv_head // kv_per, q_per + k * kv_per + kv_head % kv_per
-            ]
-
     near = [(seq + k) % seq_count for k in range(1, seq_count)]
-    for j in near:
-        send(sent.at[j, pl.ds(here, 2)], kv_ref.at[tp, seq], kv_sem.at[seq], "seq", j)
-
-    @pl.loop(0, seq_count)
-    def _(j):
-        for k in range(here):
-            head = index_ref[j * here + k]
-            sent[j, k] = landed[head // q_per, head % q_per]
-
-    for j in near:
-        send(sent.at[j, pl.ds(0, here)], q_ref.at[seq], q_sem.at[seq], "seq", j)
-    mine_kv = pltpu.make_async_copy(
-        sent.at[seq, pl.ds(here, 2)], kv_ref.at[tp, seq], local_sem.at[0]
-    )
-    mine_q = pltpu.make_async_copy(sent.at[seq, pl.ds(0, here)], q_ref.at[seq], local_sem.at[1])
-    mine_kv.start()
-    mine_q.start()
-    mine_kv.wait()
-    for n, source in enumerate([seq] + near[::-1]):
-        block = kv_ref.at[tp, source]
-        if n:
-            arrived(block, kv_sem.at[source], "seq", source)
+    mine = []
+
+    def hold(src, dst):
+        copy = pltpu.make_async_copy(src, dst, local_sem.at[1 + len(mine)])
+        copy.start()
+        mine.append(copy)
+
+    for h in range(halves):
+        rows = rows_of(h)
         for k in range(1, tp_count):
-            send(block, block, spread_sem.at[tp, source], "tp", (tp + k) % tp_count)
-    mine_q.wait()
-    for source in near:
-        arrived(q_ref.at[source], q_sem.at[source], "seq", source)
-    for k in range(1, tp_count):
-        source = (tp + k) % tp_count
-        for s in range(seq_count):
-            arrived(kv_ref.at[source, s], spread_sem.at[source, s], "tp", source)
+            source = (tp + k) % tp_count
+            arrived(landed[h].at[source], land_sem.at[source, h], "tp", source)
+
+        @pl.loop(0, seq_count)
+        def _(j):
+            kv_head = j * here // GROUP
+            for k in range(2):
+                sent[j, here + k, rows] = landed[h][
+                    kv_head // kv_per, q_per + k * kv_per + kv_head % kv_per
+                ]
+
+        for j in near:
+            send(
+                sent.at[j, pl.ds(here, 2), rows], kv_ref.at[tp, seq, :, rows],
+                kv_sem.at[seq, h], "seq", j,
+            )
+
+        @pl.loop(0, seq_count)
+        def _(j):
+            for k in range(here):
+                head = index_ref[j * here + k]
+                sent[j, k, rows] = landed[h][head // q_per, head % q_per]
+
+        for j in near:
+            send(
+                sent.at[j, pl.ds(0, here), rows], q_ref.at[seq, :, rows],
+                q_sem.at[seq, h], "seq", j,
+            )
+        hold(sent.at[seq, pl.ds(here, 2), rows], kv_ref.at[tp, seq, :, rows])
+        hold(sent.at[seq, pl.ds(0, here), rows], q_ref.at[seq, :, rows])
+
+    for copy in mine:
+        copy.wait()
+    for h in range(halves):
+        for n, source in enumerate([seq] + near[::-1]):
+            block = kv_ref.at[tp, source, :, rows_of(h)]
+            if n:
+                arrived(block, kv_sem.at[source, h], "seq", source)
+            for k in range(1, tp_count):
+                send(block, block, spread_sem.at[tp, source, h], "tp", (tp + k) % tp_count)
+    for h in range(halves):
+        for source in near:
+            arrived(q_ref.at[source, :, rows_of(h)], q_sem.at[source, h], "seq", source)
+        for k in range(1, tp_count):
+            source = (tp + k) % tp_count
+            for n in range(seq_count):
+                arrived(
+                    kv_ref.at[source, n, :, rows_of(h)], spread_sem.at[source, n, h], "tp", source
+                )
     for copy in sends:
         copy.wait_send()
 
@@ -214,7 +236,7 @@
     vmem = pl.BlockSpec(memory_space=pltpu.VMEM)
     anywhere = pl.BlockSpec(memory_space=pl.ANY)
     count = (
-        2 * chips + 2 + 2 * (chips - 1) * 3 + 2 * (seq_count - 1) + seq_count * (tp_count - 1)
+        2 * chips + 2 + 2 * (chips - 1) * 4 + 4 * (seq_count - 1) + 2 * seq_count * (tp_count - 1)
     )
     bf16 = jnp.bfloat16
     return pl.pallas_call(
@@ -229,17 +251,18 @@
             pltpu.VMEM((chips, 2, own, width), bf16),
             pltpu.VMEM((steps, width, pair * DH), bf16),
             pltpu.VMEM((chips, 2, heads, own, DH), bf16),
-            pltpu.VMEM((tp_count, heads, own, DH), bf16),
+            pltpu.VMEM((tp_count, heads, own // 2, DH), bf16),
+            pltpu.VMEM((tp_count, heads, own // 2, DH), bf16),
             pltpu.VMEM((seq_count, here + 2, own, DH), bf16),
             pltpu.VMEM((2 * own, rank), bf16),
             pltpu.SemaphoreType.DMA((steps,)),
-            pltpu.SemaphoreType.DMA((2,)),
+            pltpu.SemaphoreType.DMA((6,)),
             pltpu.SemaphoreType.DMA((count,)),
             pltpu.SemaphoreType.DMA((chips, 2, 2)),
             pltpu.SemaphoreType.DMA((tp_count, 2)),
-            pltpu.SemaphoreType.DMA((seq_count,)),
-            pltpu.SemaphoreType.DMA((seq_count,)),
-            pltpu.SemaphoreType.DMA((tp_count, seq_count)),
+            pltpu.SemaphoreType.DMA((seq_count, 2)),
+            pltpu.SemaphoreType.DMA((seq_count, 2)),
+            pltpu.SemaphoreType.DMA((tp_count, seq_count, 2)),
         ],
         compiler_params=pltpu.CompilerParams(collective_id=0, has_side_effects=True),
         name="front",

time: 135 us -> 125 us (0.926)
  Pallas kernels: 128 us -> 119 us
    pallas_call x1, Pallas kernels: 79.9 us -> 72.4 us  [front(): pl.pallas_call(functools.partial(front_kernel, rotated_heads // pair, her...]
    pallas_call x1, Pallas kernels: 19.1 us -> 17.7 us  [attend(): pl.pallas_call(functools.partial(attend_kernel, heads), grid_spec=pltpu.P...]
where the time goes in v4:
time: 125 us; the launch traced here: 126 us
  Pallas kernels  119 us (95%)
  other arithmetic  4.47 us (4%)
  local copies, waits for them, and re-layouts  2.29 us (2%)
    pallas_call x1, Pallas kernels, front(): pl.pallas_call(functools.partial(front_kernel, rotated_heads // pair, her...  72.4 us
    pallas_call x1, Pallas kernels, finish(): pl.pallas_call(finish_kernel, in_specs=[pl.BlockSpec(memory_space=pltpu.S...  28.8 us
    pallas_call x1, Pallas kernels, attend(): pl.pallas_call(functools.partial(attend_kernel, heads), grid_spec=pltpu.P...  17.7 us

profile of v4, /device:TPU:10, one launch (start us, length us, event | category | flops | bytes accessed | tf_op | source)
XLA Modules:
  0.0 125.6 jit_solution(14402694113637434766)
XLA Ops:
  0.0 0.9 convert_reduce_fusion
  0.9 0.7 multiply_add_fusion.slot_ref
  1.6 0.0 copy-start
  1.6 0.7 select_reduce_fusion.index_ref
  2.3 1.0 fusion
  3.3 1.2 select_maximum_fusion
  4.5 72.4 %front.1 = (bf16[8,4,128,128]{3,2,1,0:T(8,128)(2,1)}, bf16[4,8,2,128,128]{4,3,2,1,0:T(8,128)(2,1)}) custom-call(s32[32]{0:T(128)} %select_reduce_fusion.index_ref, bf16[128,4096]{1,0:T(8,128)(2,1)} %tokens_ref.1, bf16[4096,1536]{1,0:T(8,128)(2,1)} %w_ref.1, bf16[64,4096]{1,0:T(8,128)(2,1)} %bitcast.2, bf16[64,1536]{1,0:T(8,128)(2,1)} %up_ref.1, ...), custom_call_target="tpu_custom_call" | custom-call | tf_op jit(solution)/shard_map/front/pallas_call | solution.py:242
  76.8 17.7 %attend.1.in_ref = bf16[8,4,128,128]{3,2,1,0:T(8,128)(2,1)} custom-call(s32[4096]{0:T(1024)} %scalar_ref.1, bf16[8,4,128,128]{3,2,1,0:T(8,128)(2,1)} %get-tuple-element.7.q_ref, bf16[4,8,2,128,128]{4,3,2,1,0:T(8,128)(2,1)} %get-tuple-element.8.kv_ref, s32[32,128]{1,0:T(8,128)} %bitcast.3), custom_call_target="tpu_custom_call" | custom-call | tf_op jit(solution)/shard_map/attend/pallas_call | solution.py:371
  94.6 0.0 copy-done
  94.6 28.8 %finish.1 = bf16[128,4096]{1,0:T(8,128)(2,1)} custom-call(s32[32]{0:T(128)} %copy-done, bf16[8,4,128,128]{3,2,1,0:T(8,128)(2,1)} %attend.1.in_ref), custom_call_target="tpu_custom_call" | custom-call | tf_op jit(solution)/shard_map/finish/pallas_call | solution.py:305
  123.3 2.3 %copy.8 = bf16[128,4096]{1,0:T(8,128)(2,1)} copy(bf16[128,4096]{1,0:T(8,128)(2,1)} %finish.1) | data formatting | bytes 2097152
  (2 shorter events, 0.0 us)
Async XLA Ops:
  1.6 93.0 %copy-start = (s32[32]{0:T(128)}, s32[32]{0:T(128)S(1)}, u32[]{:S(2)}) copy-start(s32[32]{0:T(128)S(1)} %multiply_add_fusion.slot_ref) | copy-start | bytes 388

commit v5 on v4

--- a/solution.py
+++ b/solution.py
@@ -334,7 +334,7 @@
     places = jnp.concatenate([places] * heads, 0)
     factor = (DH**-0.5) * LOG2_E
 
-    def body(index, carry):
+    def body(index, carry, own_block=False):
         top, total, acc = carry
         keys = kv_ref[:, index, 0].reshape(block, DH)
         values = kv_ref[:, index, 1].reshape(block, DH)
@@ -345,7 +345,10 @@
         key_docs = jnp.concatenate(
             [doc_ref[pl.ds(index * chunks + c, 1), :] for c in range(chunks)], 1
         )
-        scores = jnp.where((at <= places) & (key_docs == docs), scores, NEG_BIG)
+        kept = key_docs == docs
+        if own_block:
+            kept = kept & (at <= places)
+        scores = jnp.where(kept, scores, NEG_BIG)
         new_top = jnp.maximum(top, jnp.max(scores, 1, keepdims=True))
         shrink = jnp.exp2((top - new_top) * factor)
         powers = jnp.exp2((scores - new_top) * factor)
@@ -361,7 +364,7 @@
         jnp.zeros((rows, 1), jnp.float32),
         jnp.zeros((rows, DH), jnp.float32),
     )
-    carry = body(last, start)
+    carry = body(last, start, True)
     top, total, acc = lax.fori_loop(first // block, last, body, carry)
     out_ref[0] = (acc / total).astype(jnp.bfloat16).reshape(heads, own, DH)
 

time: 125 us -> 124 us (level); the launches traced: 126 us -> 123 us
  Pallas kernels: 119 us -> 116 us
    pallas_call x1, Pallas kernels: 17.7 us -> 16.2 us  [attend(): pl.pallas_call(functools.partial(attend_kernel, heads), grid_spec=pltpu.P...]
where the time goes in v5:
time: 124 us; the launch traced here: 123 us
  Pallas kernels  116 us (94%)
  other arithmetic  4.47 us (4%)
  local copies, waits for them, and re-layouts  2.29 us (2%)
    pallas_call x1, Pallas kernels, front(): pl.pallas_call(functools.partial(front_kernel, rotated_heads // pair, her...  72.4 us
    pallas_call x1, Pallas kernels, finish(): pl.pallas_call(finish_kernel, in_specs=[pl.BlockSpec(memory_space=pltpu.S...  27.5 us
    pallas_call x1, Pallas kernels, attend(): pl.pallas_call(functools.partial(attend_kernel, heads), grid_spec=pltpu.P...  16.2 us

profile of v5, /device:TPU:10, one launch (start us, length us, event | category | flops | bytes accessed | tf_op | source)
XLA Modules:
  0.0 122.9 jit_solution(1460311523905552101)
XLA Ops:
  0.0 0.9 convert_reduce_fusion
  0.9 0.7 multiply_add_fusion.slot_ref
  1.6 0.0 copy-start
  1.6 0.7 select_reduce_fusion.index_ref
  2.3 1.0 fusion
  3.3 1.2 select_maximum_fusion
  4.5 72.4 %front.1 = (bf16[8,4,128,128]{3,2,1,0:T(8,128)(2,1)}, bf16[4,8,2,128,128]{4,3,2,1,0:T(8,128)(2,1)}) custom-call(s32[32]{0:T(128)} %select_reduce_fusion.index_ref, bf16[128,4096]{1,0:T(8,128)(2,1)} %tokens_ref.1, bf16[4096,1536]{1,0:T(8,128)(2,1)} %w_ref.1, bf16[64,4096]{1,0:T(8,128)(2,1)} %bitcast.2, bf16[64,1536]{1,0:T(8,128)(2,1)} %up_ref.1, ...), custom_call_target="tpu_custom_call" | custom-call | tf_op jit(solution)/shard_map/front/pallas_call | solution.py:242
  76.8 16.2 %attend.1.in_ref = bf16[8,4,128,128]{3,2,1,0:T(8,128)(2,1)} custom-call(s32[4096]{0:T(1024)} %scalar_ref.1, bf16[8,4,128,128]{3,2,1,0:T(8,128)(2,1)} %get-tuple-element.7.q_ref, bf16[4,8,2,128,128]{4,3,2,1,0:T(8,128)(2,1)} %get-tuple-element.8.kv_ref, s32[32,128]{1,0:T(8,128)} %bitcast.3), custom_call_target="tpu_custom_call" | custom-call | tf_op jit(solution)/shard_map/attend/pallas_call | solution.py:374
  93.0 0.0 copy-done
  93.0 27.5 %finish.1 = bf16[128,4096]{1,0:T(8,128)(2,1)} custom-call(s32[32]{0:T(128)} %copy-done, bf16[8,4,128,128]{3,2,1,0:T(8,128)(2,1)} %attend.1.in_ref), custom_call_target="tpu_custom_call" | custom-call | tf_op jit(solution)/shard_map/finish/pallas_call | solution.py:305
  120.6 2.3 %copy.8 = bf16[128,4096]{1,0:T(8,128)(2,1)} copy(bf16[128,4096]{1,0:T(8,128)(2,1)} %finish.1) | data formatting | bytes 2097152
  (2 shorter events, 0.0 us)
Async XLA Ops:
  1.6 91.5 %copy-start = (s32[32]{0:T(128)}, s32[32]{0:T(128)S(1)}, u32[]{:S(2)}) copy-start(s32[32]{0:T(128)S(1)} %multiply_add_fusion.slot_ref) | copy-start | bytes 388
